TPU v7x, 128 devices: a whole 4x4x4 slice. The times are simulated.
128 devices in a mesh: seq: 32 (over x, y, core), head: 4 (over z).
Axes of the slice: x: 4, y: 4, z: 4, core: 2. Of those that a mesh axis runs over, the one named last changes fastest.
Arguments:
- vis_tokens: bfloat16 [12288, 1408], P('seq'), may hold values from -70 to 70
- vis_counts: int32 [4, 8], replicated, may hold values from 1 to 384, 1536 in all within a row
- vis_spatial: int32 [4, 96], replicated, may hold values from 0 to 1023, as said below
- enc_gain: float32 [1408], replicated, may hold values from 0.25 to 1.75
- enc_bias: float32 [1408], replicated, may hold values from -3 to 3
- enc_qkv: bfloat16 [3, 1408, 1408], P(None, None, 'head'), may hold values from -6 to 6
- enc_proj: bfloat16 [1408, 1408], P('head'), may hold values from -0.15625 to 0.15625
- final_gain: float32 [1408], replicated, may hold values from 0.25 to 1.75
- final_bias: float32 [1408], replicated, may hold values from -3 to 3
- to_decoder: bfloat16 [1408, 512], replicated, may hold values from -0.15625 to 0.15625
- mask_token: float32 [512], replicated, may hold values from -4 to 4
- dec_gain: float32 [512], replicated, may hold values from 0.25 to 1.75
- dec_bias: float32 [512], replicated, may hold values from -3 to 3
- dec_qkv: bfloat16 [3, 512, 512], P(None, None, 'head'), may hold values from -11 to 11
Outputs:
- decoded: bfloat16 [4, 16, 1024, 512], P(None, None, 'seq', 'head')
Inputs may be any that keep to these rules, and one draw needn't show every extreme that they name: `vis_spatial`: row c lists in increasing order the spatial positions visible in every frame of clip c; each aligned run of 32 spatial positions holds exactly 3 of them. The visible tokens of clip c, in order of position, lie on the members of its encoder group in order, vis_counts[c, g] of them on member g; each row sums to 1536.
All inputs are finite; a program needn't handle non-finite values.
Results may differ from a plain program's by a relative error of at most 0.015.
Values may be sent and summed in bfloat16 or wider, within the bound.
A program may use at most 320 MiB of HBM per device.

v0:
```python
import math

import jax
import jax.numpy as jnp
from jax import lax
from jax.sharding import PartitionSpec as P

D = 1408
HEADS = 16
DD = 512
DHEADS = 8
S = 1024
BLOCK = 32
GROUP = 8
L = 16384
VSP = 96
VIS = 1536


epsilon = 1e-06
floor_score = -1e30


def from_partner(block, axis, distance):
    count = lax.axis_size(axis)
    route = []
    for low in range(count):
        high = low | 1 << distance
        if high != low and high < count:
            route += [(low, high), (high, low)]
    return lax.ppermute(block, axis, route)


def layer_norm(values, gain_row, bias_row):
    centre = jnp.mean(values, axis=-1, keepdims=True)
    centred = values - centre
    spread = jnp.mean(centred * centred, axis=-1, keepdims=True)
    return centred * lax.rsqrt(spread + epsilon) * gain_row + bias_row


def sinusoid(positions, table_width):
    column_ids = jnp.arange(table_width, dtype=jnp.int32)
    exponent = (2 * (column_ids // 2)).astype(jnp.float32) / table_width
    frequency = jnp.exp(exponent * -math.log(10000.0))
    angles = positions.astype(jnp.float32)[:, None] * frequency[None, :]
    return jnp.where(column_ids[None, :] % 2 == 0, jnp.sin(angles), jnp.cos(angles))


def fold_block(fold_state, queries, key_rows, value_rows, allowed, score_scale):
    running_max, running_sum, running_acc = fold_state
    scores = jnp.einsum("cqhe,ckhe->chqk", queries, key_rows, preferred_element_type=jnp.float32)
    allowed_grid = allowed[:, None, None, :]
    scores = jnp.where(allowed_grid, scores * score_scale, floor_score)
    new_max = jnp.maximum(running_max, jnp.max(scores, axis=-1))
    factor = jnp.exp(running_max - new_max)
    raised = jnp.where(allowed_grid, jnp.exp(scores - new_max[..., None]), 0.0)
    running_sum = running_sum * factor + jnp.sum(raised, axis=-1)
    weights = raised.astype(jnp.bfloat16)
    update = jnp.einsum("chqk,ckhe->chqe", weights, value_rows, preferred_element_type=jnp.float32)
    running_acc = running_acc * factor[..., None] + update
    return (new_max, running_sum, running_acc)


def empty_state(batch_count, head_count, query_count, head_size):
    return (
        jnp.full((batch_count, head_count, query_count), floor_score, jnp.float32),
        jnp.zeros((batch_count, head_count, query_count), jnp.float32),
        jnp.zeros((batch_count, head_count, query_count, head_size), jnp.float32),
    )


def body(
    vis_tokens,
    vis_counts,
    vis_spatial,
    enc_gain,
    enc_bias,
    enc_qkv,
    enc_proj,
    final_gain,
    final_bias,
    to_decoder,
    mask_token,
    dec_gain,
    dec_bias,
    dec_qkv,
):
    seq_count = lax.axis_size("seq")
    seq_index = lax.axis_index("seq")
    clips = vis_counts.shape[0]
    clip_index = seq_index % clips
    member = seq_index // clips
    slot_count = vis_tokens.shape[0]
    slot_ids = jnp.arange(slot_count, dtype=jnp.int32)
    member_ids = jnp.arange(GROUP, dtype=jnp.int32)
    group_counts = lax.dynamic_index_in_dim(vis_counts, clip_index, 0, keepdims=False)
    before = jnp.sum(jnp.where(member_ids < member, group_counts, 0))
    slot_live = slot_ids < jnp.sum(jnp.where(member_ids == member, group_counts, 0))
    token_rows = vis_tokens.astype(jnp.float32)
    normed = layer_norm(token_rows, enc_gain, enc_bias).astype(jnp.bfloat16)
    enc_parts = [
        jnp.dot(normed, enc_qkv[part_id], preferred_element_type=jnp.float32).astype(jnp.bfloat16)
        for part_id in range(3)
    ]
    head_size = D // HEADS
    enc_width = enc_parts[0].shape[1]
    local_heads = enc_width // head_size
    enc_queries = enc_parts[0].reshape(1, slot_count, local_heads, head_size)
    key_value = jnp.stack([enc_parts[1], enc_parts[2]])
    enc_scale = 1.0 / math.sqrt(head_size)
    clip_bits = clips.bit_length() - 1
    collected = key_value[None]
    for bit in range(GROUP.bit_length() - 1):
        partner = from_partner(collected, "seq", bit + clip_bits)
        upper_side = (member >> bit) % 2 == 1
        collected = jnp.where(
            upper_side,
            jnp.concatenate([partner, collected], axis=0),
            jnp.concatenate([collected, partner], axis=0),
        )
    group_keys = jnp.moveaxis(collected, 1, 0).reshape(
        2, 1, GROUP * slot_count, local_heads, head_size
    )
    group_live = (slot_ids[None, :] < group_counts[:, None]).reshape(1, GROUP * slot_count)
    fold_state = fold_block(
        empty_state(1, local_heads, slot_count, head_size),
        enc_queries,
        group_keys[0],
        group_keys[1],
        group_live,
        enc_scale,
    )
    context = fold_state[2][0] / fold_state[1][0][..., None]
    context = jnp.transpose(context, (1, 0, 2)).reshape(slot_count, enc_width).astype(jnp.bfloat16)
    partial_out = jnp.dot(context, enc_proj, preferred_element_type=jnp.float32)
    attended = lax.psum(partial_out.astype(jnp.bfloat16), "head").astype(jnp.float32)
    residual = token_rows + attended
    final_rows = layer_norm(residual, final_gain, final_bias).astype(jnp.bfloat16)
    encoded = jnp.dot(final_rows, to_decoder, preferred_element_type=jnp.float32).astype(
        jnp.bfloat16
    )
    visible_index = jnp.minimum(before + slot_ids, VIS - 1)
    spatial_row = lax.dynamic_index_in_dim(vis_spatial, clip_index, 0, keepdims=False)
    spatial_ids = jnp.arange(VSP, dtype=jnp.int32)
    spatial = jnp.sum(
        jnp.where((visible_index % VSP)[:, None] == spatial_ids[None, :], spatial_row[None, :], 0),
        axis=1,
    )
    position = visible_index // VSP * S + spatial
    block_index = position // BLOCK
    owner_index = block_index % seq_count
    own_rows = L // seq_count
    local_row = clip_index * own_rows + block_index // seq_count * BLOCK + position % BLOCK
    per_peer = slot_count // seq_count
    peer_ids = jnp.arange(seq_count, dtype=jnp.int32)
    owner_hits = ((owner_index[:, None] == peer_ids[None, :]) & slot_live[:, None]).astype(
        jnp.float32
    )
    earlier_mask = (slot_ids[None, :] < slot_ids[:, None]).astype(jnp.float32)
    earlier = jnp.dot(earlier_mask, owner_hits, precision=lax.Precision.HIGHEST)
    bucket_rank = jnp.sum(earlier * owner_hits, axis=1).astype(jnp.int32)
    target = jnp.where(slot_live, owner_index * per_peer + bucket_rank, -1)
    bucket_ids = jnp.arange(seq_count * per_peer, dtype=jnp.int32)
    chosen = target[None, :] == bucket_ids[:, None]
    send_rows = (
        jnp.dot(chosen.astype(jnp.bfloat16), encoded, preferred_element_type=jnp.float32)
        .astype(jnp.bfloat16)
        .reshape(seq_count, per_peer, DD)
    )
    send_index = jnp.max(jnp.where(chosen, local_row[None, :], -1), axis=1).reshape(
        seq_count, per_peer
    )
    got_rows, got_index = (
        lax.all_to_all(send_rows, "seq", split_axis=0, concat_axis=0, tiled=True),
        lax.all_to_all(send_index, "seq", split_axis=0, concat_axis=0, tiled=True),
    )
    total_rows = clips * own_rows
    got_index = jnp.where(got_index < 0, total_rows, got_index).reshape(-1)
    placed = (
        jnp.zeros((total_rows, DD), jnp.float32)
        .at[got_index]
        .set(got_rows.reshape(-1, DD).astype(jnp.float32), mode="drop")
    )
    row_ids = jnp.arange(own_rows, dtype=jnp.int32)
    local_position = (row_ids // BLOCK * seq_count + seq_index) * BLOCK + row_ids % BLOCK
    frame_ids = jnp.arange(S, dtype=jnp.int32)
    spatial_flags = jnp.any(vis_spatial[:, :, None] == frame_ids[None, None, :], axis=1)
    column_pick = ((local_position % S)[:, None] == frame_ids[None, :]).astype(jnp.float32)
    seen_flags = (
        jnp.einsum(
            "cs,rs->cr",
            spatial_flags.astype(jnp.float32),
            column_pick,
            precision=lax.Precision.HIGHEST,
        )
        > 0.5
    )
    inputs = sinusoid(local_position, DD)[None] + jnp.where(
        seen_flags[..., None], placed.reshape(clips, own_rows, DD), mask_token[None, None, :]
    )
    dec_normed = layer_norm(inputs, dec_gain, dec_bias).astype(jnp.bfloat16)
    dec_size = DD // DHEADS
    dec_query = jnp.einsum(
        "crd,de->cre", dec_normed, dec_qkv[0], preferred_element_type=jnp.float32
    ).astype(jnp.bfloat16)
    dec_width = dec_query.shape[2]
    dec_heads = dec_width // dec_size
    dec_queries = dec_query.reshape(clips, own_rows, dec_heads, dec_size)
    dec_scale = 1.0 / math.sqrt(dec_size)
    start_state = empty_state(clips, dec_heads, own_rows, dec_size)
    dec_key = jnp.einsum(
        "crd,de->cre", dec_normed, dec_qkv[1], preferred_element_type=jnp.float32
    ).astype(jnp.bfloat16)
    dec_value = jnp.einsum(
        "crd,de->cre", dec_normed, dec_qkv[2], preferred_element_type=jnp.float32
    ).astype(jnp.bfloat16)
    stacked = jnp.stack([dec_key, dec_value])
    shard_part = lax.all_gather(stacked, "seq", axis=2, tiled=True)
    row_count = shard_part.shape[2]
    block_count = row_count // own_rows
    block_rows = row_count // block_count
    grouped = jnp.moveaxis(
        shard_part.reshape(2, clips, block_count, block_rows, dec_heads, dec_size), 2, 0
    )
    everywhere = jnp.ones((clips, block_rows), dtype=bool)

    def scan_step(inner_state, key_block):
        return (
            fold_block(inner_state, dec_queries, key_block[0], key_block[1], everywhere, dec_scale),
            None,
        )

    result_state, _ = lax.scan(scan_step, start_state, grouped)
    fold_state = result_state
    dec_context = fold_state[2] / fold_state[1][..., None]
    dec_context = jnp.transpose(dec_context, (0, 2, 1, 3)).reshape(
        clips, own_rows // BLOCK, BLOCK, dec_width
    )
    return dec_context.astype(jnp.bfloat16)


def solution(mesh):
    in_specs = (
        P("seq", None),
        P(),
        P(),
        P(),
        P(),
        P(None, None, "head"),
        P("head", None),
        P(),
        P(),
        P(),
        P(),
        P(),
        P(),
        P(None, None, "head"),
    )
    out_specs = P(None, None, "seq", "head")
    return jax.shard_map(body, mesh=mesh, in_specs=in_specs, out_specs=out_specs, check_vma=False)
```

profile of v0, /device:TPU:1, one launch (start us, length us, event | category | flops | bytes accessed | tf_op | source)
XLA Modules:
  0.0 682.1 jit_solution(31880487049167066)
XLA Ops:
  14.1 3.8 collective-permute-start
  17.9 11.9 %collective-permute-done = bf16[1,2,384,352]{2,3,1,0:T(8,128)(2,1)} collective-permute-done((bf16[1,2,384,352]{2,3,1,0:T(8,128)(2,1)S(1)}, bf16[1,2,384,352]{2,3,1,0:T(8,128)(2,1)}, u32[]{:S(2)}, u32[]{:S(2)}) %collective-permute-start) | collective-permute-done | bytes 540704 | tf_op jit(solution)/shard_map/ppermute | solution.py:31
  33.3 23.1 %collective-permute-done.1 = bf16[2,2,384,352]{2,3,1,0:T(8,128)(2,1)} collective-permute-done((bf16[2,2,384,352]{2,3,1,0:T(8,128)(2,1)}, bf16[2,2,384,352]{2,3,1,0:T(8,128)(2,1)}, u32[]{:S(2)}, u32[]{:S(2)}) %collective-permute-start.1) | collective-permute-done | bytes 1081376 | tf_op jit(solution)/shard_map/ppermute | solution.py:31
  56.4 4.0 maximum_select_fusion.1
  68.0 40.4 %collective-permute-done.2 = bf16[4,2,384,352]{2,3,1,0:T(8,128)(2,1)} collective-permute-done((bf16[4,2,384,352]{2,3,1,0:T(8,128)(2,1)}, bf16[4,2,384,352]{2,3,1,0:T(8,128)(2,1)}, u32[]{:S(2)}, u32[]{:S(2)}) %collective-permute-start.2) | collective-permute-done | bytes 2162720 | tf_op jit(solution)/shard_map/ppermute | solution.py:31
  108.5 3.9 fusion.22
  116.3 4.2 reshape.477
  120.6 3.7 copy.37
  124.2 4.4 reshape.478
  128.6 11.2 %fusion.16 = (f32[4,384]{1,0:T(4,128)S(1)}, f32[4,384,3072]{2,1,0:T(8,128)}) fusion(pred[3072]{0:T(1024)(128)(4,1)S(1)} %lt.153, bf16[384,4,88]{0,2,1:T(8,128)(2,1)S(1)} %bitcast.138, bf16[3072,4,88]{0,2,1:T(8,128)(2,1)} %reshape.477), kind=kOutput, calls=%fused_computation.24 | convolution fusion | flops 844626432 | bytes 21316608 | tf_op jit(solution)/shard_map/cqhe,ckhe->chqk/dot_general | solution.py:51
  139.9 11.2 %fusion.17 = f32[4,384]{1,0:T(4,128)S(1)} fusion(f32[4,384,3072]{2,1,0:T(8,128)} %get-tuple-element.105, f32[4,384]{1,0:T(4,128)S(1)} %get-tuple-element.103, pred[3072]{0:T(1024)(128)(4,1)S(1)} %lt.153), kind=kLoop, calls=%fused_computation.25 | loop fusion | flops 23591424 | bytes 18889728 | tf_op jit(solution)/shard_map/reduce_sum | solution.py:57
  151.1 12.2 %fusion.62 = bf16[384,4,88]{0,2,1:T(8,128)(2,1)} fusion(bf16[3072,4,88]{0,2,1:T(8,128)(2,1)} %reshape.478, f32[4,384,3072]{2,1,0:T(8,128)} %get-tuple-element.105, f32[4,384]{1,0:T(4,128)S(1)} %get-tuple-element.103, pred[3072]{0:T(1024)(128)(4,1)S(1)} %lt.153, f32[384,4]{0,1:T(4,128)S(1)} %bitcast_add_fusion.1, f32[384,4]{0,1:T(4,128)S(1)} %get-tuple-element.102), kind=kOutput, calls=%fused_computation.86 | convolution fusion | flops 854470656 | bytes 21328896 | tf_op jit(solution)/shard_map/chqk,ckhe->chqe/dot_general | solution.py:59
  168.5 10.2 %all-to-all-start = ((s32[32,1,12]{2,1,0:T(1,128)}), s32[32,1,12]{2,1,0:T(1,128)S(1)}, u32[]{:S(2)}, u32[]{:S(2)}) async-start(s32[32,1,12]{2,1,0:T(1,128)} %bitcast.3), calls=%async_computation | async-start | bytes 32768 | tf_op jit(solution)/shard_map/all_to_all | solution.py:175
  179.6 36.2 %all-reduce.2.cloned.1.call-done = bf16[384,1408]{1,0:T(8,128)(2,1)} async-done(((bf16[384,1408]{1,0:T(8,128)(2,1)}), bf16[384,1408]{1,0:T(8,128)(2,1)}) %all-reduce.2.cloned.1.call-update) | async-done | bytes 1081360 | tf_op jit(solution)/shard_map/psum | solution.py:136
  221.3 9.3 %all-to-all-start.1 = ((bf16[32,12,512]{2,1,0:T(8,128)(2,1)}), bf16[32,12,512]{2,1,0:T(8,128)(2,1)S(1)}, u32[]{:S(2)}, u32[]{:S(2)}) async-start(bf16[32,12,512]{2,1,0:T(8,128)(2,1)} %reshape.479), calls=%async_computation.1 | async-start | bytes 1048576 | tf_op jit(solution)/shard_map/all_to_all | solution.py:174
  230.7 3.7 fusion.57
  235.9 6.3 all-to-all-done.1
  242.3 4.0 scatter_custom_fusion
  246.3 3.1 fusion.23
  257.3 108.5 %all-gather.2.cloned.1.call-done = bf16[2,4,16384,128]{3,2,1,0:T(8,128)(2,1)} async-done(((bf16[2,4,512,128]{3,2,1,0:T(8,128)(2,1)}), bf16[2,4,16384,128]{3,2,1,0:T(8,128)(2,1)}) %all-gather.2.cloned.1.call-update) | async-done | bytes 33554448 | tf_op jit(solution)/shard_map/all_gather | solution.py:218
  365.8 44.1 %copy.38 = bf16[2,4,16384,128]{2,3,1,0:T(8,128)(2,1)} copy(bf16[2,4,16384,128]{3,2,1,0:T(8,128)(2,1)} %all-gather.2.cloned.1.call-done) | data formatting | bytes 67108864 | tf_op jit(solution)/shard_map/all_gather | solution.py:218
  409.9 22.7 %copy.45 = bf16[128,8,32,512]{3,2,1,0:T(8,128)(2,1)} copy(bf16[128,8,32,512]{3,1,2,0:T(8,128)(2,1)} %bitcast.132) | data formatting | bytes 67108864
  432.6 22.9 %copy.40 = bf16[32,2,4,512,2,64]{3,5,4,2,1,0:T(8,128)(2,1)} copy(bf16[32,2,4,512,2,64]{3,0,5,4,2,1:T(8,128)(2,1)} %bitcast.133) | data formatting | bytes 67108864
  455.5 217.1 %while.15 = (s32[]{:T(128)}, f32[4,2,512]{2,1,0:T(2,128)S(1)}, f32[4,2,512]{2,1,0:T(2,128)S(1)}, f32[4,2,512,64]{2,3,1,0:T(8,128)S(1)}, bf16[32,2,4,512,2,64]{3,...) while((s32[]{:T(128)}, f32[4,2,512]{2,1,0:T(2,128)S(1)}, ...), condition=%wide.region_19.20_spmd.clone, body=%wide.region_16.19_spmd.clone.sunk | while | flops 554455040 | bytes 29098120 | solution.py:233
  473.0 2.9 fusion.145
  493.3 2.9 fusion.145
  520.5 2.9 fusion.145
  540.8 2.9 fusion.145
  567.9 2.9 fusion.145
  588.3 2.9 fusion.145
  615.4 2.9 fusion.145
  635.8 2.9 fusion.145
  (282 shorter events, 238.0 us)
Async XLA Ops:
  6.5 211.5 %copy-start = (bf16[1408,512]{1,0:T(8,128)(2,1)S(1)}, bf16[1408,512]{1,0:T(8,128)(2,1)}, u32[]{:S(2)}) copy-start(bf16[1408,512]{1,0:T(8,128)(2,1)} %param.25) | copy-start | bytes 4325380
  6.5 3.3 copy-start.4
  6.5 3.3 copy-start.12
  6.5 3.3 copy-start.13
  6.5 209.3 %all-reduce.2.cloned.1.call-start = ((), (), s32[]{:S(2)}) async-start(), calls=%async_computation.2 | async-start | bytes 2162688 | tf_op jit(solution)/shard_map/psum | solution.py:136
  14.1 15.7 %collective-permute-start = (bf16[1,2,384,352]{2,3,1,0:T(8,128)(2,1)S(1)}, bf16[1,2,384,352]{2,3,1,0:T(8,128)(2,1)}, u32[]{:S(2)}, u32[]{:S(2)}) collective-permute-start(bf16[1,2,384,352]{2,3,1,0:T(8,128)(2,1)S(1)} %maximum_bitcast_fusion), channel_id=1, source_target_pairs={{0,16},{16,0},{4,20},{20,4},{8,24},{24,8},{12,28},{28,12},{32,48},... | collective-permute-start | bytes 1622024 | tf_op jit(solution)/shard_map/ppermute | solution.py:31
  32.2 24.3 %collective-permute-start.1 = (bf16[2,2,384,352]{2,3,1,0:T(8,128)(2,1)}, bf16[2,2,384,352]{2,3,1,0:T(8,128)(2,1)}, u32[]{:S(2)}, u32[]{:S(2)}) collective-permute-start(bf16[2,2,384,352]{2,3,1,0:T(8,128)(2,1)} %maximum_select_fusion.2), channel_id=1, source_target_pairs={{0,32},{32,0},{4,36},{36,4},{8,40},{40,8},{12,44},{44,12},{16,48},... | collective-permute-start | bytes 3244040 | tf_op jit(solution)/shard_map/ppermute | solution.py:31
  33.3 31.1 %copy-start.11 = (s32[4,96]{1,0:T(4,128)S(1)}, s32[4,96]{1,0:T(4,128)}, u32[]{:S(2)}) copy-start(s32[4,96]{1,0:T(4,128)} %param.18) | copy-start | bytes 4612
  60.4 48.1 %collective-permute-start.2 = (bf16[4,2,384,352]{2,3,1,0:T(8,128)(2,1)}, bf16[4,2,384,352]{2,3,1,0:T(8,128)(2,1)}, u32[]{:S(2)}, u32[]{:S(2)}) collective-permute-start(bf16[4,2,384,352]{2,3,1,0:T(8,128)(2,1)} %maximum_select_fusion.1), channel_id=1, source_target_pairs={{0,64},{64,0},{4,68},{68,4},{8,72},{72,8},{12,76},{76,12},{16,80},... | collective-permute-start | bytes 6488072 | tf_op jit(solution)/shard_map/ppermute | solution.py:31
  151.1 12.2 %copy-start.6 = (bf16[352,1408]{1,0:T(8,128)(2,1)S(1)}, bf16[352,1408]{1,0:T(8,128)(2,1)}, u32[]{:S(2)}) copy-start(bf16[352,1408]{1,0:T(8,128)(2,1)} %param.22) | copy-start | bytes 2973700
  168.5 52.8 %all-to-all-start = ((s32[32,1,12]{2,1,0:T(1,128)}), s32[32,1,12]{2,1,0:T(1,128)S(1)}, u32[]{:S(2)}, u32[]{:S(2)}) async-start(s32[32,1,12]{2,1,0:T(1,128)} %bitcast.3), calls=%async_computation | async-start | bytes 32768 | tf_op jit(solution)/shard_map/all_to_all | solution.py:175
  179.6 38.5 %copy-start.14 = (f32[1408]{0:T(1024)S(1)}, f32[1408]{0:T(1024)}, u32[]{:S(2)}) copy-start(f32[1408]{0:T(1024)} %param.24) | copy-start | bytes 16900
  179.6 38.5 %copy-start.15 = (f32[1408]{0:T(1024)S(1)}, f32[1408]{0:T(1024)}, u32[]{:S(2)}) copy-start(f32[1408]{0:T(1024)} %param.23) | copy-start | bytes 16900
  215.8 1.7 copy-start.5
  221.3 20.9 %all-to-all-start.1 = ((bf16[32,12,512]{2,1,0:T(8,128)(2,1)}), bf16[32,12,512]{2,1,0:T(8,128)(2,1)S(1)}, u32[]{:S(2)}, u32[]{:S(2)}) async-start(bf16[32,12,512]{2,1,0:T(8,128)(2,1)} %reshape.479), calls=%async_computation.1 | async-start | bytes 1048576 | tf_op jit(solution)/shard_map/all_to_all | solution.py:174
  230.6 135.2 %all-gather.2.cloned.1.call-start = ((), (), s32[]{:S(2)}) async-start(), calls=%async_computation.3 | async-start | bytes 34603008 | tf_op jit(solution)/shard_map/all_gather | solution.py:218
  242.3 4.0 copy-start.8
  246.3 3.4 copy-start.2
  249.7 1.3 copy-start.9
  249.7 1.3 copy-start.10
  251.1 1.2 copy-start.7
  252.3 1.4 copy-start.3
  672.6 2.2 copy-start.1
Sparse Core Ops, SparseCore 0:
  166.2 49.5 all-reduce.1
  255.0 110.8 all-gather.1
where the time goes:
time: 693 us; the launch traced here: 682 us
  waiting for transfers between devices  226 us (33%)
  matrix products  207 us (30%)
  local copies, waits for them, and re-layouts  115 us (17%)
  other arithmetic  90.5 us (13%)
  starting transfers between devices  27.2 us (4%)
  between operations  14.3 us (2%)
    all_gather x1, waiting for transfers between devices, body(): shard_part = lax.all_gather(stacked, 'seq', axis=2, tiled=True)  109 us
    dot_general x33, matrix products, fold_block(): jnp.einsum('chqk,ckhe->chqe', weights, value_rows, preferred_element_type...  105 us
    dot_general x33, matrix products, fold_block(): jnp.einsum('cqhe,ckhe->chqk', queries, key_rows, preferred_element_type=j...  86.7 us
    ppermute x3, waiting for transfers between devices, from_partner(): return lax.ppermute(block, axis, route)  75.4 us
    reduce_sum x33, other arithmetic, fold_block(): running_sum = running_sum * factor + jnp.sum(raised, axis=-1)  56.9 us
    unnamed x35, local copies, waits for them, and re-layouts  46.1 us
    all_gather x1, local copies, waits for them, and re-layouts, body(): shard_part = lax.all_gather(stacked, 'seq', axis=2, tiled=True)  44.1 us
    psum x1, waiting for transfers between devices, body(): lax.psum(partial_out.astype(jnp.bfloat16), 'head').astype(jnp.float32)  36.2 us
  transfers between devices with their start and end apart: 7, of which 6 were waited for; matrix products, arithmetic and copies ran while one was open for 3% of the time, Pallas kernels for 0%

commit v1 on v0

v1 whole, which is shorter than its diff:
```python
import math

import jax
import jax.numpy as jnp
from jax import lax
from jax.experimental import pallas as pl
from jax.experimental.pallas import tpu as pltpu
from jax.sharding import PartitionSpec as P

D = 1408
HEADS = 16
DD = 512
DHEADS = 8
S = 1024
BLOCK = 32
VB = 3
GROUP = 8
L = 16384
VSP = 96
VIS = 1536
FRAMES = L // S
CLIPS = 4
SLOTS = 384
QUARTER = 96
CHUNK = 128
CHUNKS = S // CHUNK
KEYS = CHUNK * FRAMES
OWN = FRAMES * BLOCK
OWNVIS = FRAMES * VB
HEAD = DD // DHEADS
LOG2E = 1.4426950408889634
epsilon = 1e-06
floor_score = -1e30
NT = (((1,), (1,)), ((), ()))


def layer_norm(values, gain_row, bias_row):
    centre = jnp.mean(values, axis=-1, keepdims=True)
    centred = values - centre
    spread = jnp.mean(centred * centred, axis=-1, keepdims=True)
    return centred * lax.rsqrt(spread + epsilon) * gain_row + bias_row


def frequencies():
    column_ids = jnp.arange(DD, dtype=jnp.int32)
    exponent = (2 * (column_ids // 2)).astype(jnp.float32) / DD
    return column_ids % 2 == 0, jnp.exp(exponent * -math.log(10000.0))


def sinusoid(positions):
    even, frequency = frequencies()
    angles = positions.astype(jnp.float32)[:, None] * frequency[None, :]
    return jnp.where(even[None, :], jnp.sin(angles), jnp.cos(angles))


TILES = 8


def table_kernel(a1, a2, b1, b2, token, gain, bias, wkv, keep, k_ref, v_ref):
    lanes = lax.broadcasted_iota(jnp.int32, (1, 2 * HEAD), 1)
    for tile in range(TILES):
        rows = pl.ds(tile * CHUNK, CHUNK)
        x = a1[0, tile : tile + 1, :] * b1[...] + a2[0, tile : tile + 1, :] * b2[...] + token[...]
        h = layer_norm(x, gain[...], bias[...]).astype(jnp.bfloat16)
        kv = jnp.dot(h, wkv[...], preferred_element_type=jnp.float32)
        k_ref[rows, :] = kv[:, : 2 * HEAD].astype(jnp.bfloat16)
        v = kv[:, 2 * HEAD :]
        turned = pltpu.roll(v, HEAD, 1)
        for head in range(2):
            twice = jnp.where((lanes < HEAD) == (head == 0), v, turned)
            v_ref[head, rows, :] = (jnp.concatenate([twice, twice], axis=1) * keep[0]).astype(jnp.bfloat16)


def angle_tables(coarse, fine):
    even, frequency = frequencies()
    angle_a = coarse.astype(jnp.float32)[:, None] * frequency[None, :]
    angle_b = fine.astype(jnp.float32)[:, None] * frequency[None, :]
    sin_a, cos_a = jnp.sin(angle_a), jnp.cos(angle_a)
    a1 = jnp.where(even[None, :], sin_a, cos_a)
    a2 = jnp.where(even[None, :], cos_a, -sin_a)
    return lax.optimization_barrier((a1, a2, jnp.cos(angle_b), jnp.sin(angle_b)))


def make_tables(mask_token, dec_gain, dec_bias, wkv, keep):
    coarse = (jnp.arange(FRAMES) * S)[None, :] + (jnp.arange(CHUNKS) * CHUNK)[:, None]
    a1, a2, b1, b2 = angle_tables(coarse.reshape(-1), jnp.arange(CHUNK))
    a1, a2 = a1.reshape(-1, TILES, DD), a2.reshape(-1, TILES, DD)
    steps = a1.shape[0]
    per_chunk = steps // CHUNKS
    whole = lambda *shape: pl.BlockSpec(shape, lambda i: (0,) * len(shape))
    return pl.pallas_call(
        table_kernel,
        grid=(steps,),
        in_specs=[
            pl.BlockSpec((1, TILES, DD), lambda i: (i, 0, 0)),
            pl.BlockSpec((1, TILES, DD), lambda i: (i, 0, 0)),
            whole(CHUNK, DD),
            whole(CHUNK, DD),
            whole(1, DD),
            whole(1, DD),
            whole(1, DD),
            whole(DD, 4 * HEAD),
            pl.BlockSpec((1, CHUNK, CLIPS * HEAD), lambda i: (i // per_chunk, 0, 0)),
        ],
        out_specs=[
            pl.BlockSpec((TILES * CHUNK, 2 * HEAD), lambda i: (i, 0)),
            pl.BlockSpec((2, TILES * CHUNK, CLIPS * HEAD), lambda i: (0, i, 0)),
        ],
        out_shape=[
            jax.ShapeDtypeStruct((L, 2 * HEAD), jnp.bfloat16),
            jax.ShapeDtypeStruct((2, L, CLIPS * HEAD), jnp.bfloat16),
        ],
        cost_estimate=pl.CostEstimate(flops=20 * 10**9, bytes_accessed=25 * 10**6, transcendentals=0),
        name="masked_tables",
    )(a1, a2, b1, b2, mask_token[None], dec_gain[None], dec_bias[None], wkv, keep)


def lane_tiles(x):
    total = x[:, :CHUNK]
    for tile in range(1, x.shape[1] // CHUNK):
        total = total + x[:, tile * CHUNK : (tile + 1) * CHUNK]
    return total


BASE_ROWS = 128
JOIN_ROWS = 512


def base_kernel(q_ref, k_ref, v_ref, keep_ref, acc_ref, m_ref, l_ref):
    first = pl.program_id(1) == 0

    @pl.when(first)
    def _():
        acc_ref[...] = jnp.zeros_like(acc_ref)
        l_ref[...] = jnp.zeros_like(l_ref)
        m_ref[...] = jnp.full_like(m_ref, floor_score)

    for start in range(0, OWN, BASE_ROWS):
        rows = pl.ds(start, BASE_ROWS)
        s = lax.dot_general(q_ref[0, rows, :], k_ref[...], NT, preferred_element_type=jnp.float32)
        old = m_ref[0, rows, :]
        new = jnp.maximum(old, jnp.max(s, axis=1, keepdims=True))
        factor = jnp.exp2((old - new) * LOG2E)
        e = jnp.exp2((s - new[:, :1]) * LOG2E)
        total = lane_tiles(e)
        for clip in range(CLIPS):
            l_ref[0, clip, rows, :] = l_ref[0, clip, rows, :] * factor + total * keep_ref[0, clip : clip + 1, :]
        m_ref[0, rows, :] = new
        update = jnp.dot(e.astype(jnp.bfloat16), v_ref[0], preferred_element_type=jnp.float32)
        acc_ref[0, rows, :] = acc_ref[0, rows, :] * jnp.concatenate([factor, factor], axis=1) + update


def base_attention(q, k, v4, keep_rows):
    return pl.pallas_call(
        base_kernel,
        grid=(2, CHUNKS),
        in_specs=[
            pl.BlockSpec((1, OWN, 2 * HEAD), lambda h, j: (h, 0, 0)),
            pl.BlockSpec((KEYS, 2 * HEAD), lambda h, j: (j, 0)),
            pl.BlockSpec((1, KEYS, CLIPS * HEAD), lambda h, j: (h, j, 0)),
            pl.BlockSpec((1, CLIPS, CHUNK), lambda h, j: (j, 0, 0)),
        ],
        out_specs=[
            pl.BlockSpec((1, OWN, CLIPS * HEAD), lambda h, j: (h, 0, 0)),
            pl.BlockSpec((1, OWN, CHUNK), lambda h, j: (h, 0, 0)),
            pl.BlockSpec((1, CLIPS, OWN, CHUNK), lambda h, j: (h, 0, 0, 0)),
        ],
        out_shape=[
            jax.ShapeDtypeStruct((2, OWN, CLIPS * HEAD), jnp.float32),
            jax.ShapeDtypeStruct((2, OWN, CHUNK), jnp.float32),
            jax.ShapeDtypeStruct((2, CLIPS, OWN, CHUNK), jnp.float32),
        ],
        cost_estimate=pl.CostEstimate(flops=25 * 10**9, bytes_accessed=25 * 10**6, transcendentals=17 * 10**6),
        name="masked_queries",
    )(q, k, v4, keep_rows)


def single_kernel(q_ref, k_ref, v_ref, offset_ref, acc_ref, m_ref, l_ref):
    @pl.when(pl.program_id(1) == 0)
    def _():
        acc_ref[...] = jnp.zeros_like(acc_ref)
        l_ref[...] = jnp.zeros_like(l_ref)
        m_ref[...] = jnp.full_like(m_ref, floor_score)

    offset = jnp.concatenate([offset_ref[0]] * FRAMES, axis=1)
    for head in range(2):
        s = lax.dot_general(q_ref[head], k_ref[...], NT, preferred_element_type=jnp.float32) + offset
        old = m_ref[head]
        new = jnp.maximum(old, jnp.max(s, axis=1, keepdims=True))
        factor = jnp.exp2((old - new) * LOG2E)
        e = jnp.exp2((s - new[:, :1]) * LOG2E)
        l_ref[head] = l_ref[head] * factor + lane_tiles(e)
        m_ref[head] = new
        update = jnp.dot(e.astype(jnp.bfloat16), v_ref[head], preferred_element_type=jnp.float32)
        acc_ref[head] = acc_ref[head] * jnp.concatenate([factor, factor], axis=1) + update


def single_attention(q, k, v4, offsets, block):
    rows = q.shape[1]
    blocks = rows // block
    offset_map = (lambda r, j: (j, r, 0)) if offsets.shape[1] == rows else (lambda r, j: (j, 0, 0))
    out_spec = lambda width: pl.BlockSpec((2, block, width), lambda r, j: (0, r, 0))
    return pl.pallas_call(
        single_kernel,
        grid=(blocks, CHUNKS),
        in_specs=[
            pl.BlockSpec((2, block, 2 * HEAD), lambda r, j: (0, r, 0)),
            pl.BlockSpec((KEYS, 2 * HEAD), lambda r, j: (j, 0)),
            pl.BlockSpec((2, KEYS, CLIPS * HEAD), lambda r, j: (0, j, 0)),
            pl.BlockSpec((1, block, CHUNK), offset_map),
        ],
        out_specs=[out_spec(CLIPS * HEAD), out_spec(CHUNK), out_spec(CHUNK)],
        out_shape=[
            jax.ShapeDtypeStruct((2, rows, CLIPS * HEAD), jnp.float32),
            jax.ShapeDtypeStruct((2, rows, CHUNK), jnp.float32),
            jax.ShapeDtypeStruct((2, rows, CHUNK), jnp.float32),
        ],
        cost_estimate=pl.CostEstimate(flops=20 * 10**9, bytes_accessed=25 * 10**6, transcendentals=6 * 10**6),
        name="visible_queries" if blocks == 1 else "masked_queries_by_clip",
    )(q, k, v4, offsets)


def own_columns(acc, clip, head):
    piece = jnp.where(clip >= 2, acc[:, CHUNK:], acc[:, :CHUNK])
    return jnp.where(clip % 2 == head, piece, pltpu.roll(piece, HEAD, 1))


def join(q, k, v, acc, m, l):
    s = lax.dot_general(q, k, NT, preferred_element_type=jnp.float32)
    new = jnp.maximum(m, jnp.max(s, axis=1, keepdims=True))
    e = jnp.exp2((s - new[:, :1]) * LOG2E)
    factor = jnp.exp2((m - new) * LOG2E)
    total = jnp.sum(l * factor + lane_tiles(e), axis=1, keepdims=True)
    update = jnp.dot(e.astype(jnp.bfloat16), v, preferred_element_type=jnp.float32)
    return (acc * factor + update) / total


def join_kernel(qb_ref, qv_ref, kv_ref, accb_ref, mb_ref, lb_ref, accv_ref, mv_ref, lv_ref, place_ref, out_ref):
    clip = pl.program_id(0)
    lanes = lax.broadcasted_iota(jnp.int32, (1, 2 * HEAD), 1)
    k = kv_ref[:, 0, :, : 2 * HEAD].reshape(VIS, 2 * HEAD)
    v = kv_ref[:, 0, :, 2 * HEAD :].reshape(VIS, 2 * HEAD)
    place = place_ref[0]
    seen = jnp.sum(place, axis=1, keepdims=True) > 0.5
    for head in range(2):
        mine = (lanes // HEAD) == head
        vis = join(
            qv_ref[head, 0], k, v, own_columns(accv_ref[head, 0], clip, head), mv_ref[head, 0], lv_ref[head, 0]
        ).astype(jnp.bfloat16)
        for start in range(0, OWN, JOIN_ROWS):
            rows = pl.ds(start, JOIN_ROWS)
            base = join(
                qb_ref[head, rows, :],
                k,
                v,
                own_columns(accb_ref[head, rows, :], clip, head),
                mb_ref[head, 0, rows, :],
                lb_ref[head, 0, rows, :],
            )
            spread = jnp.dot(
                place[start : start + JOIN_ROWS].astype(jnp.bfloat16), vis, preferred_element_type=jnp.float32
            )
            value = jnp.where(seen[start : start + JOIN_ROWS], spread, base).astype(jnp.bfloat16)
            if head == 0:
                out_ref[0, rows, :] = value
            else:
                out_ref[0, rows, :] = jnp.where(mine, value, out_ref[0, rows, :])


def join_attention(qb, qv, kv, base, single, place):
    seq_count = kv.shape[0]
    accb, mb, lb = base
    accv, mv, lv = [x.reshape(2, CLIPS, OWNVIS, -1) for x in single]
    vis_spec = lambda width: pl.BlockSpec((2, 1, OWNVIS, width), lambda c: (0, c, 0, 0))
    return pl.pallas_call(
        join_kernel,
        grid=(CLIPS,),
        in_specs=[
            pl.BlockSpec((2, OWN, 2 * HEAD), lambda c: (0, 0, 0)),
            vis_spec(2 * HEAD),
            pl.BlockSpec((seq_count, 1, OWNVIS, 4 * HEAD), lambda c: (0, c, 0, 0)),
            pl.BlockSpec((2, OWN, CLIPS * HEAD), lambda c: (0, 0, 0)),
            pl.BlockSpec((2, 1, OWN, CHUNK), lambda c: (0, c, 0, 0)),
            pl.BlockSpec((2, 1, OWN, CHUNK), lambda c: (0, c, 0, 0)),
            vis_spec(CLIPS * HEAD),
            vis_spec(CHUNK),
            vis_spec(CHUNK),
            pl.BlockSpec((1, OWN, OWNVIS), lambda c: (c, 0, 0)),
        ],
        out_specs=pl.BlockSpec((1, OWN, 2 * HEAD), lambda c: (c, 0, 0)),
        out_shape=jax.ShapeDtypeStruct((CLIPS, OWN, 2 * HEAD), jnp.bfloat16),
        cost_estimate=pl.CostEstimate(flops=8 * 10**9, bytes_accessed=10**7, transcendentals=7 * 10**6),
        name="join_visible_keys",
    )(qb, qv.reshape(2, CLIPS, OWNVIS, -1), kv, accb, mb, lb, accv, mv, lv, place)


def project_kernel(x_ref, gain_ref, bias_ref, w_ref, q_ref, kv_ref, h_ref):
    part = pl.program_id(0)

    @pl.when(part == 0)
    def _():
        h_ref[...] = layer_norm(x_ref[...].astype(jnp.float32), gain_ref[...], bias_ref[...]).astype(jnp.bfloat16)

    value = lax.dot_general(h_ref[...], w_ref[0], NT, preferred_element_type=jnp.float32).astype(jnp.bfloat16)

    @pl.when(part == 2)
    def _():
        q_ref[...] = value

    @pl.when(part < 2)
    def _():
        kv_ref[0] = value


def encoder_projections(x, gain, bias, w):
    slots, width = x.shape[0], w.shape[1]
    return pl.pallas_call(
        project_kernel,
        grid=(3,),
        in_specs=[
            pl.BlockSpec((slots, D), lambda i: (0, 0)),
            pl.BlockSpec((1, D), lambda i: (0, 0)),
            pl.BlockSpec((1, D), lambda i: (0, 0)),
            pl.BlockSpec((1, width, D), lambda i: ((i + 1) % 3, 0, 0)),
        ],
        out_specs=[
            pl.BlockSpec((slots, width), lambda i: (0, 0)),
            pl.BlockSpec((1, slots, width), lambda i: (jnp.minimum(i, 1), 0, 0)),
        ],
        out_shape=[
            jax.ShapeDtypeStruct((slots, width), jnp.bfloat16),
            jax.ShapeDtypeStruct((2, slots, width), jnp.bfloat16),
        ],
        scratch_shapes=[pltpu.VMEM((slots, D), jnp.bfloat16)],
        cost_estimate=pl.CostEstimate(flops=12 * 10**8, bytes_accessed=5 * 10**6, transcendentals=0),
        name="encoder_projections",
    )(x, gain[None], bias[None], w)


def encoder_kernel(q_ref, kv_ref, offset_ref, out_ref):
    width = q_ref.shape[1]
    head_size = D // HEADS
    k = kv_ref[:, 0].reshape(GROUP * SLOTS, width)
    v = kv_ref[:, 1].reshape(GROUP * SLOTS, width)
    scale = LOG2E / math.sqrt(head_size)
    sums = []
    for low, high, heads in ((0, 256, (0, 1)), (128, width, (2, 3))):
        lanes = lax.broadcasted_iota(jnp.int32, (1, high - low), 1) + low
        window = q_ref[:, low:high]
        result = None
        for head in heads:
            mine = (lanes >= head * head_size) & (lanes < (head + 1) * head_size)
            q = jnp.where(mine, window, jnp.zeros_like(window))
            s = lax.dot_general(q, k[:, low:high], NT, preferred_element_type=jnp.float32) * scale + offset_ref[...]
            e = jnp.exp2(s - jnp.max(s, axis=1, keepdims=True))
            total = jnp.sum(lane_tiles(e), axis=1, keepdims=True)
            context = jnp.dot(e.astype(jnp.bfloat16), v[:, low:high], preferred_element_type=jnp.float32)
            context = jnp.where(mine, context / total, 0.0)
            result = context if result is None else result + context
        sums.append(result)
    out_ref[:, :128] = sums[0][:, :128].astype(jnp.bfloat16)
    out_ref[:, 128:256] = (sums[0][:, 128:] + sums[1][:, :128]).astype(jnp.bfloat16)
    out_ref[:, 256:] = sums[1][:, 128:].astype(jnp.bfloat16)


def encoder_attention(q, kv, offset):
    return pl.pallas_call(
        encoder_kernel,
        in_specs=[pl.BlockSpec(memory_space=pltpu.VMEM)] * 3,
        out_specs=pl.BlockSpec(memory_space=pltpu.VMEM),
        out_shape=jax.ShapeDtypeStruct(q.shape, jnp.bfloat16),
        cost_estimate=pl.CostEstimate(flops=9 * 10**9, bytes_accessed=5 * 10**6, transcendentals=5 * 10**6),
        name="encoder_attention",
    )(q, kv, offset)


def body(
    vis_tokens,
    vis_counts,
    vis_spatial,
    enc_gain,
    enc_bias,
    enc_qkv,
    enc_proj,
    final_gain,
    final_bias,
    to_decoder,
    mask_token,
    dec_gain,
    dec_bias,
    dec_qkv,
):
    seq_count = lax.axis_size("seq")
    seq_index = lax.axis_index("seq")
    quarter = lax.axis_index("head")
    clip_index = seq_index % CLIPS
    member = seq_index // CLIPS
    slot_ids = jnp.arange(SLOTS, dtype=jnp.int32)
    starts = jnp.cumsum(vis_counts, axis=1) - vis_counts
    group_counts = lax.dynamic_index_in_dim(vis_counts, clip_index, 0, keepdims=False)
    before = lax.dynamic_slice(starts, (clip_index, member), (1, 1))[0, 0]

    enc_q, enc_kv = encoder_projections(vis_tokens, enc_gain, enc_bias, jnp.swapaxes(enc_qkv, 1, 2))
    groups = [[clip + CLIPS * g for g in range(GROUP)] for clip in range(CLIPS)]
    group_kv = lax.all_gather(enc_kv, "seq", axis_index_groups=groups)
    live = (slot_ids[None, :] < group_counts[:, None]).reshape(1, GROUP * SLOTS)

    frame_ids = jnp.arange(S, dtype=jnp.int32)
    flags = jnp.any(vis_spatial[:, :, None] == frame_ids[None, None, :], axis=1)
    kept = jnp.where(flags, 0.0, 1.0)
    keep_rows = kept.reshape(CLIPS, CHUNKS, CHUNK).transpose(1, 0, 2)
    lane_clip = jnp.arange(CLIPS * HEAD, dtype=jnp.int32) // HEAD
    clip_lanes = (lane_clip[None, :] == jnp.arange(CLIPS)[:, None]).astype(jnp.float32)
    keep = jnp.dot(kept.T, clip_lanes, precision=lax.Precision.HIGHEST).reshape(CHUNKS, CHUNK, CLIPS * HEAD)
    offset_rows = (1.0 - keep_rows) * floor_score
    offsets = jnp.repeat(offset_rows, OWNVIS, axis=1)
    wkv = jnp.concatenate([dec_qkv[1], dec_qkv[2]], axis=1)
    k_masked, v_masked = make_tables(mask_token, dec_gain, dec_bias, wkv, keep)

    own_ids = jnp.arange(OWN, dtype=jnp.int32)
    own_frame, own_place = own_ids // BLOCK, own_ids % BLOCK
    scale = 1.0 / math.sqrt(HEAD)
    head_of_lane = jnp.arange(2 * HEAD, dtype=jnp.int32) // HEAD

    def split_heads(q):
        q = (q.astype(jnp.bfloat16) * jnp.bfloat16(scale))[None]
        return jnp.where(jnp.arange(2)[:, None, None] == head_of_lane[None, None, :], q, jnp.bfloat16(0))

    own_spatial = lax.dynamic_slice(vis_spatial, (0, seq_index * VB), (CLIPS, VB))
    fine = jnp.concatenate([seq_index * BLOCK + jnp.arange(BLOCK, dtype=jnp.int32), own_spatial.reshape(-1)])
    a1, a2, b1, b2 = angle_tables(jnp.arange(FRAMES, dtype=jnp.int32) * S, fine)
    own_table = a1[:, None, :] * b1[None, :BLOCK] + a2[:, None, :] * b2[None, :BLOCK]
    own_table = own_table.reshape(OWN, DD) + mask_token[None, :]
    base_in = layer_norm(own_table, dec_gain, dec_bias).astype(jnp.bfloat16)
    q_masked = split_heads(jnp.dot(base_in, dec_qkv[0], preferred_element_type=jnp.float32))
    b1, b2 = b1[BLOCK:].reshape(CLIPS, 1, VB, DD), b2[BLOCK:].reshape(CLIPS, 1, VB, DD)
    vis_table = a1[None, :, None, :] * b1 + a2[None, :, None, :] * b2
    base = base_attention(q_masked, k_masked, v_masked, keep_rows)
    source = (slot_ids - before) % SLOTS
    turn = (source[:, None] == slot_ids[None, :]).astype(jnp.bfloat16)
    turn_part = lax.dynamic_slice_in_dim(turn, quarter * QUARTER, QUARTER, 0)
    tokens_part = jnp.dot(turn_part, vis_tokens, preferred_element_type=jnp.float32)
    group_kv, base, tokens_part, vis_table, turn = lax.optimization_barrier(
        (group_kv, base, tokens_part, vis_table, turn)
    )

    def by_clip(_):
        offset = jnp.broadcast_to(
            offset_rows.transpose(1, 0, 2)[:, :, None, :], (CLIPS, CHUNKS, BASE_ROWS, CHUNK)
        )
        accs, ms, ls = lax.map(lambda x: single_attention(q_masked, k_masked, v_masked, x, BASE_ROWS), offset)
        acc = accs[0]
        for clip in range(1, CLIPS):
            acc = jnp.where(lane_clip[None, None, :] == clip, accs[clip], acc)
        return acc, jnp.swapaxes(ms, 0, 1), jnp.swapaxes(ls, 0, 1)

    def shared(_):
        return base[0], jnp.broadcast_to(base[1][:, None], (2, CLIPS, OWN, CHUNK)), base[2]

    vanishing = jnp.min(jnp.sum(base[2], axis=-1)) < 2.0**-60
    base = lax.cond(vanishing, by_clip, shared, None)

    context = encoder_attention(enc_q, group_kv, jnp.where(live, 0.0, floor_score))
    turned = jnp.dot(turn, context, preferred_element_type=jnp.float32).astype(jnp.bfloat16)
    partial_out = jnp.dot(turned, enc_proj, preferred_element_type=jnp.float32).astype(jnp.bfloat16)
    attended = lax.psum_scatter(partial_out, "head", scatter_dimension=0, tiled=True).astype(jnp.float32)
    final_rows = layer_norm(tokens_part + attended, final_gain, final_bias).astype(jnp.bfloat16)
    encoded = jnp.dot(final_rows, to_decoder, preferred_element_type=jnp.float32).astype(jnp.bfloat16)

    arrived = lax.all_to_all(encoded.reshape(seq_count, VB, DD), "seq", split_axis=0, concat_axis=0, tiled=True)
    arrived = lax.all_gather(arrived, "head")
    a_ids = jnp.arange(4, dtype=jnp.int32)[:, None, None]
    from_ids = jnp.arange(seq_count, dtype=jnp.int32)
    i_ids = jnp.arange(VB, dtype=jnp.int32)[None, None, :]
    from_start = starts.T.reshape(-1)[None, :, None]
    from_count = vis_counts.T.reshape(-1)[None, :, None]
    row = a_ids * VSP + seq_index * VB + i_ids
    offset_in = (row - from_start) % SLOTS
    token = from_start + offset_in
    frame = token // VSP
    target = (from_ids % CLIPS)[None, :, None] * OWNVIS + frame * VB + i_ids
    target = jnp.where(offset_in < from_count, target, -1).reshape(-1)
    pick = (jnp.arange(CLIPS * OWNVIS, dtype=jnp.int32)[:, None] == target[None, :]).astype(jnp.bfloat16)
    own_encoded = jnp.dot(pick, arrived.reshape(-1, DD), preferred_element_type=jnp.float32)

    vis_in = vis_table.reshape(CLIPS * OWNVIS, DD) + own_encoded
    vis_in = layer_norm(vis_in, dec_gain, dec_bias).astype(jnp.bfloat16)
    vis_q, vis_k, vis_v = [jnp.dot(vis_in, dec_qkv[i], preferred_element_type=jnp.float32) for i in range(3)]
    vis_kv = jnp.concatenate([vis_k, vis_v], axis=1).astype(jnp.bfloat16).reshape(CLIPS, OWNVIS, 4 * HEAD)
    all_kv = lax.all_gather(vis_kv, "seq")
    q_visible = split_heads(vis_q)
    single = single_attention(q_visible, k_masked, v_masked, offsets, CLIPS * OWNVIS)

    token_ids = jnp.arange(OWNVIS, dtype=jnp.int32)
    token_place = jnp.repeat(own_spatial[:, None, :] - seq_index * BLOCK, FRAMES, axis=1).reshape(CLIPS, 1, OWNVIS)
    place = (own_frame[None, :, None] == (token_ids // VB)[None, None, :]) & (own_place[None, :, None] == token_place)
    place = place.astype(jnp.float32)

    out = join_attention(q_masked, q_visible, all_kv, base, single, place)
    return out.reshape(CLIPS, FRAMES, BLOCK, 2 * HEAD)


def solution(mesh):
    in_specs = (
        P("seq", None),
        P(),
        P(),
        P(),
        P(),
        P(None, None, "head"),
        P("head", None),
        P(),
        P(),
        P(),
        P(),
        P(),
        P(),
        P(None, None, "head"),
    )
    out_specs = P(None, None, "seq", "head")
    return jax.shard_map(body, mesh=mesh, in_specs=in_specs, out_specs=out_specs, check_vma=False)
```

time: 693 us -> 242 us (0.35); the launches traced: 682 us -> 241 us
  matrix products: 207 us -> 10 us
  waiting for transfers between devices: 226 us -> 50.8 us
  Pallas kernels: 0 us -> 112 us
  local copies, waits for them, and re-layouts: 115 us -> 19.5 us
  other arithmetic: 90.5 us -> 15.7 us
  starting transfers between devices: 27.2 us -> 9.24 us
  blocking collectives: 0 us -> 9.86 us
    dot_general x76 -> x9, matrix products: 207 us -> 10 us  [the longest x1 3.47 us: body(): jnp.dot(turned, enc_proj, preferred_element_type=jnp.float32)]
    pallas_call x0 -> x6, Pallas kernels: none -> 112 us  [the longest x1 35 us: base_attention(): pl.pallas_call(base_kernel, grid=(2, CHUNKS), in_specs=[pl.BlockSpec((1,...]
    all_gather x1 -> x2, waiting for transfers between devices: 109 us -> 23.7 us  [the longest x1 18.3 us: body(): all_kv = lax.all_gather(vis_kv, 'seq')]
    ppermute x3 -> x0, waiting for transfers between devices: 75.4 us -> none  [from_partner(): return lax.ppermute(block, axis, route)]
    reduce_sum x35 -> x1, other arithmetic: 58.3 us -> 0.62 us  [body(): vanishing = jnp.min(jnp.sum(base[2], axis=-1)) < 2.0 ** (-60)]
    unnamed x35 -> x37, local copies, waits for them, and re-layouts: 46.1 us -> 0.69 us
    all_gather x1 -> x2, local copies, waits for them, and re-layouts: 44.1 us -> 6.86 us  [the longest x1 6.52 us: body(): group_kv = lax.all_gather(enc_kv, 'seq', axis_index_groups=groups)]
    psum x1 -> x0, waiting for transfers between devices: 36.2 us -> none  [body(): lax.psum(partial_out.astype(jnp.bfloat16), 'head').astype(jnp.float32)]
  transfers between devices with their start and end apart: 7 -> 4, of which waited for: 6 -> 4; matrix products, arithmetic and copies ran while one was open for 3% -> 9% of each run, Pallas kernels for 0% -> 31%
where the time goes in v1:
time: 242 us; the launch traced here: 241 us
  Pallas kernels  112 us (46%)
  waiting for transfers between devices  50.8 us (21%)
  local copies, waits for them, and re-layouts  19.5 us (8%)
  other arithmetic  15.7 us (6%)
  between operations  14.4 us (6%)
  matrix products  10 us (4%)
  blocking collectives  9.86 us (4%)
  starting transfers between devices  9.24 us (4%)
    pallas_call x1, Pallas kernels, base_attention(): pl.pallas_call(base_kernel, grid=(2, CHUNKS), in_specs=[pl.BlockSpec((1,...  35 us
    pallas_call x1, Pallas kernels, make_tables(): pl.pallas_call(table_kernel, grid=(steps,), in_specs=[pl.BlockSpec((1, TI...  22.5 us
    pallas_call x1, Pallas kernels, join_attention(): pl.pallas_call(join_kernel, grid=(CLIPS,), in_specs=[pl.BlockSpec((2, OWN...  19.7 us
    reduce_scatter x1, waiting for transfers between devices, body(): lax.psum_scatter(partial_out, 'head', scatter_dimension=0, tiled=True)  19.6 us
    all_gather x1, waiting for transfers between devices, body(): all_kv = lax.all_gather(vis_kv, 'seq')  18.3 us
    pallas_call x1, Pallas kernels, single_attention(): pl.pallas_call(single_kernel, grid=(blocks, CHUNKS), in_specs=[pl.BlockSp...  17.4 us
    pallas_call x1, Pallas kernels, encoder_attention(): pl.pallas_call(encoder_kernel, in_specs=[pl.BlockSpec(memory_space=pltpu....  11.3 us
    all_gather x1, blocking collectives, body(): arrived = lax.all_gather(arrived, 'head')  9.86 us
  transfers between devices with their start and end apart: 4, of which 4 were waited for; matrix products, arithmetic and copies ran while one was open for 9% of the time, Pallas kernels for 31%

profile of v1, /device:TPU:1, one launch (start us, length us, event | category | flops | bytes accessed | tf_op | source)
XLA Modules:
  0.0 241.5 jit_solution(9551908164360399586)
XLA Ops:
  6.5 1.4 broadcast_in_dim.219.gain_ref
  7.9 1.3 broadcast_in_dim.220.bias_ref
  9.2 6.1 %encoder_projections.1 = (bf16[384,352]{1,0:T(8,128)(2,1)}, bf16[2,384,352]{2,1,0:T(8,128)(2,1)}) custom-call(bf16[384,1408]{1,0:T(8,128)(2,1)} %x_ref.1, f32[1,1408]{1,0:T(1,128)} %broadcast_in_dim.219.gain_ref, f32[1,1408]{1,0:T(1,128)} %broadcast_in_dim.220.bias_ref, bf16[3,352,1408]{2,1,0:T(8,128)(2,1)} %bitcast.109), custom_call_target="tpu_custom_call" | custom-call | flops 1200000000 | bytes 5000000 | tf_op jit(solution)/shard_map/encoder_projections/pallas_call | solution.py:317
  15.3 2.2 copy.37
  18.8 2.8 %multiply_sine_fusion = (f32[128,512]{1,0:T(8,128)}, f32[128,512]{1,0:T(8,128)}, f32[128,512]{1,0:T(8,128)}, f32[128,512]{1,0:T(8,128)}) fusion(f32[128]{0:T(128)S(1)} %iota_convert_fusion, f32[512]{0:T(512)S(1)} %fusion.46, f32[128]{0:T(128)S(1)} %convert_element_type.121, pred[512]{0:T(512)(128)(4,1)S(1)} %fusion.41), kind=kLoop, calls=%fused_computation.41 | loop fusion | flops 327680 | bytes 1052160 | tf_op jit(solution)/shard_map/sin | solution.py:81
  23.9 0.8 pad_maximum_fusion.wkv
  26.9 0.7 broadcast_select_fusion.q_ref.qb_ref
  27.9 1.6 fusion.34
  29.8 22.5 %masked_tables.1 = (bf16[16384,128]{1,0:T(8,128)(2,1)}, bf16[2,16384,256]{2,1,0:T(8,128)(2,1)}) custom-call(f32[16,8,512]{2,1,0:T(8,128)} %bitcast.100, f32[16,8,512]{2,1,0:T(8,128)} %bitcast.101, f32[128,512]{1,0:T(8,128)} %get-tuple-element.139.b1, f32[128,512]{1,0:T(8,128)} %get-tuple-element.140.b2, f32[1,512]{1,0:T(1,128)} %bitcast.103, ...), custom_call_target="tpu_custom_call" | custom-call | flops 20000000000 | bytes 25000000 | tf_op jit(solution)/shard_map/masked_tables/pallas_call | solution.py:91
  52.3 35.0 %masked_queries.1 = (f32[2,512,256]{2,1,0:T(8,128)}, f32[2,512,128]{2,1,0:T(8,128)}, f32[2,4,512,128]{3,2,1,0:T(8,128)}) custom-call(bf16[2,512,128]{2,1,0:T(8,128)(2,1)} %broadcast_select_fusion.q_ref.qb_ref, bf16[16384,128]{1,0:T(8,128)(2,1)} %get-tuple-element.141.k_ref, bf16[2,16384,256]{2,1,0:T(8,128)(2,1)} %get-tuple-element.142.v_ref, ...), custom_call_target="tpu_custom_call" | custom-call | flops 24999999488 | bytes 25000000 | tf_op jit(solution)/shard_map/masked_queries/pallas_call | solution.py:154
  87.3 5.4 %all-gather.7.cloned.1.call-done = bf16[16,384,352]{1,2,0:T(8,128)(2,1)} async-done(((bf16[2,384,352]{1,2,0:T(8,128)(2,1)}), bf16[16,384,352]{1,2,0:T(8,128)(2,1)}) %all-gather.7.cloned.1.call-update) | async-done | bytes 4325392 | tf_op jit(solution)/shard_map/all_gather | solution.py:405
  92.8 6.5 %copy.38 = bf16[16,384,352]{2,1,0:T(8,128)(2,1)} copy(bf16[16,384,352]{1,2,0:T(8,128)(2,1)} %all-gather.7.cloned.1.call-done) | data formatting | bytes 8650752 | tf_op jit(solution)/shard_map/all_gather | solution.py:405
  99.3 11.3 %encoder_attention.1 = bf16[384,352]{1,0:T(8,128)(2,1)} custom-call(bf16[384,352]{1,0:T(8,128)(2,1)} %get-tuple-element.149.q_ref, bf16[8,2,384,352]{3,2,1,0:T(8,128)(2,1)} %bitcast.91, f32[1,3072]{1,0:T(1,128)} %bitcast.105), custom_call_target="tpu_custom_call" | custom-call | flops 8999999488 | bytes 5000000 | tf_op jit(solution)/shard_map/encoder_attention/pallas_call | solution.py:367
  110.5 3.5 %convolution_convert_fusion = bf16[384,1408]{1,0:T(8,128)(2,1)} fusion(bf16[352,1408]{1,0:T(8,128)(2,1)} %param.24, bf16[384,384]{1,0:T(8,128)(2,1)S(1)} %get-tuple-element.148, bf16[384,352]{1,0:T(8,128)(2,1)} %encoder_attention.1), kind=kOutput, calls=%fused_computation.14 | convolution fusion | flops 485117952 | bytes 2637824 | tf_op jit(solution)/shard_map/dot_general | solution.py:465
  115.8 19.6 %reduce-scatter.2.cloned.1.call-done = bf16[96,1408]{1,0:T(8,128)(2,1)} async-done(((bf16[384,1408]{1,0:T(8,128)(2,1)}), bf16[96,1408]{1,0:T(8,128)(2,1)}) %reduce-scatter.2.cloned.1.call-update) | async-done | bytes 270352 | tf_op jit(solution)/shard_map/reduce_scatter | solution.py:466
  135.4 1.1 fusion.19
  136.5 1.2 multiply_reduce_fusion.1
  137.7 1.4 convolution_convert_fusion.3
  139.1 0.7 reshape.623
  139.9 9.2 %all-to-all-start = ((bf16[32,3,512]{2,1,0:T(4,128)(2,1)}), bf16[32,3,512]{2,1,0:T(4,128)(2,1)S(1)}, u32[]{:S(2)}, u32[]{:S(2)}) async-start(bf16[32,3,512]{2,1,0:T(4,128)(2,1)} %reshape.623), calls=%async_computation.1 | async-start | bytes 262144 | tf_op jit(solution)/shard_map/all_to_all | solution.py:470
  149.3 7.4 %all-to-all-done = bf16[32,3,512]{2,1,0:T(4,128)(2,1)S(1)} async-done(((bf16[32,3,512]{2,1,0:T(4,128)(2,1)}), bf16[32,3,512]{2,1,0:T(4,128)(2,1)S(1)}, u32[]{:S(2)}, u32[]{:S(2)}) %all-to-all-start) | async-done | bytes 98336 | tf_op jit(solution)/shard_map/all_to_all | solution.py:470
  156.7 9.9 %all-gather.1 = bf16[128,3,512]{2,0,1:T(8,128)(2,1)S(1)} all-gather(bf16[32,3,512]{2,0,1:T(8,128)(2,1)S(1)} %copy.41), channel_id=3, replica_groups=mesh['seq'=32,'head'=4] {'head'}, dimensions={0}, use_global_device_ids=true | all-gather | bytes 491520 | tf_op jit(solution)/shard_map/all_gather | solution.py:471
  166.9 1.1 reshape.624
  168.0 1.5 fusion.62
  171.3 1.3 and_convert_fusion.place_ref
  174.6 1.5 conditional.1
  174.6 1.5 broadcast_in_dim.110.clone
  176.1 1.1 fusion.9
  178.5 1.0 broadcast_in_dim.235
  179.5 17.4 %visible_queries.1 = (f32[2,192,256]{2,1,0:T(8,128)}, f32[2,192,128]{2,1,0:T(8,128)}, f32[2,192,128]{2,1,0:T(8,128)}) custom-call(bf16[2,192,128]{2,1,0:T(8,128)(2,1)} %broadcast_select_fusion.1.q_ref, bf16[16384,128]{1,0:T(8,128)(2,1)} %get-tuple-element.141.k_ref, bf16[2,16384,256]{2,1,0:T(8,128)(2,1)} %get-tuple-element.142.v_ref, f32[8,192,128]{2,1,0:T(8,128)} %bitcast.98), custom_call_target="tpu_custom_call" | custom-call | flops 20000000000 | bytes 25000000 | tf_op jit(solution)/shard_map/visible_queries/pallas_call | solution.py:203
  197.0 18.3 %all-gather.5.cloned.1.call-done.kv_ref = bf16[32,4,48,256]{3,2,1,0:T(8,128)(2,1)} async-done(((bf16[1,4,48,256]{3,2,1,0:T(8,128)(2,1)}), bf16[32,4,48,256]{3,2,1,0:T(8,128)(2,1)}) %all-gather.5.cloned.1.call-update) | async-done | bytes 3145744 | tf_op jit(solution)/shard_map/all_gather | solution.py:490
  215.2 19.7 %join_visible_keys.1 = bf16[4,512,128]{2,1,0:T(8,128)(2,1)} custom-call(bf16[2,512,128]{2,1,0:T(8,128)(2,1)} %broadcast_select_fusion.q_ref.qb_ref, bf16[2,4,48,128]{3,2,1,0:T(8,128)(2,1)} %broadcast_select_fusion.2.qv_ref, bf16[32,4,48,256]{3,2,1,0:T(8,128)(2,1)} %all-gather.5.cloned.1.call-done.kv_ref, f32[2,512,256]{2,1,0:T(8,128)} %get-tuple-element.154.accb_ref, ...), custom_call_target="tpu_custom_call" | custom-call | flops 8000000000 | bytes 10000000 | tf_op jit(solution)/shard_map/join_visible_keys/pallas_call | solution.py:275
  (127 shorter events, 12.8 us)
Async XLA Ops:
  6.5 131.2 %copy-start = (bf16[1408,512]{1,0:T(8,128)(2,1)S(1)}, bf16[1408,512]{1,0:T(8,128)(2,1)}, u32[]{:S(2)}) copy-start(bf16[1408,512]{1,0:T(8,128)(2,1)} %param.27) | copy-start | bytes 4325380
  6.5 86.2 %all-gather.7.cloned.1.call-start = ((), (), s32[]{:S(2)}) async-start(), calls=%async_computation.4 | async-start | bytes 4866048 | tf_op jit(solution)/shard_map/all_gather | solution.py:405
  9.2 8.4 %copy-start.18 = (s32[4,96]{1,0:T(4,128)S(1)}, s32[4,96]{1,0:T(4,128)}, u32[]{:S(2)}) copy-start(s32[4,96]{1,0:T(4,128)} %param.20) | copy-start | bytes 4612
  15.3 6.4 %copy-start.11 = (s32[4,8]{1,0:T(4,128)S(1)}, s32[4,8]{1,0:T(4,128)}, u32[]{:S(2)}) copy-start(s32[4,8]{1,0:T(4,128)} %param.19) | copy-start | bytes 388
  15.3 8.5 %copy-start.6 = (bf16[3,512,128]{2,1,0:T(8,128)(2,1)S(1)}, bf16[3,512,128]{2,1,0:T(8,128)(2,1)}, u32[]{:S(2)}) copy-start(bf16[3,512,128]{2,1,0:T(8,128)(2,1)} %param.31) | copy-start | bytes 1179652
  17.5 7.5 %copy-start.10 = (f32[512]{0:T(512)S(1)}, f32[512]{0:T(512)}, u32[]{:S(2)}) copy-start(f32[512]{0:T(512)} %param.28) | copy-start | bytes 6148
  17.5 8.8 %copy-start.14 = (f32[512]{0:T(512)S(1)}, f32[512]{0:T(512)}, u32[]{:S(2)}) copy-start(f32[512]{0:T(512)} %param.30) | copy-start | bytes 6148
  17.5 8.8 %copy-start.16 = (f32[512]{0:T(512)S(1)}, f32[512]{0:T(512)}, u32[]{:S(2)}) copy-start(f32[512]{0:T(512)} %param.29) | copy-start | bytes 6148
  17.5 117.9 %reduce-scatter.2.cloned.1.call-start = ((), (), s32[]{:S(2)}) async-start(), calls=%async_computation.2 | async-start | bytes 1351680 | tf_op jit(solution)/shard_map/reduce_scatter | solution.py:466
  25.6 3.9 %copy-start.8 = (bf16[384,1408]{1,0:T(8,128)(2,1)S(1)}, bf16[384,1408]{1,0:T(8,128)(2,1)}, u32[]{:S(2)}) copy-start(bf16[384,1408]{1,0:T(8,128)(2,1)} %x_ref.1) | copy-start | bytes 3244036
  25.6 3.9 %copy-start.19 = (pred[2,128]{1,0:T(4,128)(4,1)}, pred[2,128]{1,0:T(4,128)(4,1)S(1)}, u32[]{:S(2)}) copy-start(pred[2,128]{1,0:T(4,128)(4,1)S(1)} %iota_compare_fusion.7) | copy-start | bytes 772
  114.0 23.7 %copy-start.12 = (f32[1408]{0:T(1024)S(1)}, f32[1408]{0:T(1024)}, u32[]{:S(2)}) copy-start(f32[1408]{0:T(1024)} %param.26) | copy-start | bytes 16900
  114.0 23.7 %copy-start.13 = (f32[1408]{0:T(1024)S(1)}, f32[1408]{0:T(1024)}, u32[]{:S(2)}) copy-start(f32[1408]{0:T(1024)} %param.25) | copy-start | bytes 16900
  139.9 16.8 %all-to-all-start = ((bf16[32,3,512]{2,1,0:T(4,128)(2,1)}), bf16[32,3,512]{2,1,0:T(4,128)(2,1)S(1)}, u32[]{:S(2)}, u32[]{:S(2)}) async-start(bf16[32,3,512]{2,1,0:T(4,128)(2,1)} %reshape.623), calls=%async_computation.1 | async-start | bytes 262144 | tf_op jit(solution)/shard_map/all_to_all | solution.py:470
  149.0 66.2 %all-gather.5.cloned.1.call-start = ((), (), s32[]{:S(2)}) async-start(), calls=%async_computation.3 | async-start | bytes 3244032 | tf_op jit(solution)/shard_map/all_gather | solution.py:490
  149.3 20.4 %copy-start.15 = (f32[512]{0:T(512)S(1)}, f32[512]{0:T(512)}, u32[]{:S(2)}) copy-start(f32[512]{0:T(512)} %param.30) | copy-start | bytes 6148
  149.3 20.4 %copy-start.17 = (f32[512]{0:T(512)S(1)}, f32[512]{0:T(512)}, u32[]{:S(2)}) copy-start(f32[512]{0:T(512)} %param.29) | copy-start | bytes 6148
  166.6 3.3 %copy-start.7 = (bf16[3,512,128]{2,1,0:T(8,128)(2,1)S(1)}, bf16[3,512,128]{2,1,0:T(8,128)(2,1)}, u32[]{:S(2)}) copy-start(bf16[3,512,128]{2,1,0:T(8,128)(2,1)} %param.31) | copy-start | bytes 1179652
  168.0 4.6 %copy-start.3 = (f32[2,4,512,128]{3,2,1,0:T(8,128)S(1)}, f32[2,4,512,128]{3,2,1,0:T(8,128)}, u32[]{:S(2)}) copy-start(f32[2,4,512,128]{3,2,1,0:T(8,128)} %get-tuple-element.151) | copy-start | bytes 6291460
  170.3 4.3 %copy-start.9 = (f32[2,512,128]{2,1,0:T(8,128)S(1)}, f32[2,512,128]{2,1,0:T(8,128)}, u32[]{:S(2)}) copy-start(f32[2,512,128]{2,1,0:T(8,128)} %get-tuple-element.152) | copy-start | bytes 1572868
  174.6 2.6 %copy-start.20 = (pred[2,128]{1,0:T(4,128)(4,1)S(1)}, pred[2,128]{1,0:T(4,128)(4,1)}, u32[]{:S(2)}) copy-start(pred[2,128]{1,0:T(4,128)(4,1)} %copy-done.19) | copy-start | bytes 772
  215.2 19.7 %copy-start.1 = (bf16[1408,512]{1,0:T(8,128)(2,1)S(1)}, bf16[1408,512]{1,0:T(8,128)(2,1)}, u32[]{:S(2)}) copy-start(bf16[1408,512]{1,0:T(8,128)(2,1)} %param.27) | copy-start | bytes 4325380
Sparse Core Ops, SparseCore 0:
  17.6 75.0 all-gather.6
  114.2 21.1 reduce-scatter.1
  171.1 44.0 all-gather.4

commit v2 on v1

--- a/solution.py
+++ b/solution.py
@@ -299,17 +299,16 @@
 
     @pl.when(part == 0)
     def _():
-        h_ref[...] = layer_norm(x_ref[...].astype(jnp.float32), gain_ref[...], bias_ref[...]).astype(jnp.bfloat16)
-
-    value = lax.dot_general(h_ref[...], w_ref[0], NT, preferred_element_type=jnp.float32).astype(jnp.bfloat16)
+        gain, bias = gain_ref[...].reshape(1, D), bias_ref[...].reshape(1, D)
+        h_ref[...] = layer_norm(x_ref[...].astype(jnp.float32), gain, bias).astype(jnp.bfloat16)
 
     @pl.when(part == 2)
     def _():
-        q_ref[...] = value
+        q_ref[...] = lax.dot_general(h_ref[...], w_ref[0], NT, preferred_element_type=jnp.float32).astype(jnp.bfloat16)
 
     @pl.when(part < 2)
     def _():
-        kv_ref[0] = value
+        kv_ref[0] = lax.dot_general(w_ref[0], h_ref[...], NT, preferred_element_type=jnp.float32).astype(jnp.bfloat16)
 
 
 def encoder_projections(x, gain, bias, w):
@@ -319,29 +318,27 @@
         grid=(3,),
         in_specs=[
             pl.BlockSpec((slots, D), lambda i: (0, 0)),
-            pl.BlockSpec((1, D), lambda i: (0, 0)),
-            pl.BlockSpec((1, D), lambda i: (0, 0)),
+            pl.BlockSpec((D,), lambda i: (0,)),
+            pl.BlockSpec((D,), lambda i: (0,)),
             pl.BlockSpec((1, width, D), lambda i: ((i + 1) % 3, 0, 0)),
         ],
         out_specs=[
             pl.BlockSpec((slots, width), lambda i: (0, 0)),
-            pl.BlockSpec((1, slots, width), lambda i: (jnp.minimum(i, 1), 0, 0)),
+            pl.BlockSpec((1, width, slots), lambda i: (jnp.minimum(i, 1), 0, 0)),
         ],
         out_shape=[
             jax.ShapeDtypeStruct((slots, width), jnp.bfloat16),
-            jax.ShapeDtypeStruct((2, slots, width), jnp.bfloat16),
+            jax.ShapeDtypeStruct((2, width, slots), jnp.bfloat16),
         ],
         scratch_shapes=[pltpu.VMEM((slots, D), jnp.bfloat16)],
         cost_estimate=pl.CostEstimate(flops=12 * 10**8, bytes_accessed=5 * 10**6, transcendentals=0),
         name="encoder_projections",
-    )(x, gain[None], bias[None], w)
-
-
-def encoder_kernel(q_ref, kv_ref, offset_ref, out_ref):
+    )(x, gain, bias, w)
+
+
+def encoder_kernel(q_ref, kv_ref, offset_ref, turn_ref, out_ref, context_ref):
     width = q_ref.shape[1]
     head_size = D // HEADS
-    k = kv_ref[:, 0].reshape(GROUP * SLOTS, width)
-    v = kv_ref[:, 1].reshape(GROUP * SLOTS, width)
     scale = LOG2E / math.sqrt(head_size)
     sums = []
     for low, high, heads in ((0, 256, (0, 1)), (128, width, (2, 3))):
@@ -351,27 +348,168 @@
         for head in heads:
             mine = (lanes >= head * head_size) & (lanes < (head + 1) * head_size)
             q = jnp.where(mine, window, jnp.zeros_like(window))
-            s = lax.dot_general(q, k[:, low:high], NT, preferred_element_type=jnp.float32) * scale + offset_ref[...]
+            s = [jnp.dot(q, kv_ref[g, 0, low:high, :], preferred_element_type=jnp.float32) for g in range(GROUP)]
+            s = jnp.concatenate(s, axis=1) * scale + offset_ref[...]
             e = jnp.exp2(s - jnp.max(s, axis=1, keepdims=True))
             total = jnp.sum(lane_tiles(e), axis=1, keepdims=True)
-            context = jnp.dot(e.astype(jnp.bfloat16), v[:, low:high], preferred_element_type=jnp.float32)
+            e = e.astype(jnp.bfloat16)
+            context = None
+            for g in range(GROUP):
+                piece = lax.dot_general(
+                    e[:, g * SLOTS : (g + 1) * SLOTS],
+                    kv_ref[g, 1, low:high, :],
+                    NT,
+                    preferred_element_type=jnp.float32,
+                )
+                context = piece if context is None else context + piece
             context = jnp.where(mine, context / total, 0.0)
             result = context if result is None else result + context
         sums.append(result)
-    out_ref[:, :128] = sums[0][:, :128].astype(jnp.bfloat16)
-    out_ref[:, 128:256] = (sums[0][:, 128:] + sums[1][:, :128]).astype(jnp.bfloat16)
-    out_ref[:, 256:] = sums[1][:, 128:].astype(jnp.bfloat16)
-
-
-def encoder_attention(q, kv, offset):
+    context_ref[:, :128] = sums[0][:, :128].astype(jnp.bfloat16)
+    context_ref[:, 128:256] = (sums[0][:, 128:] + sums[1][:, :128]).astype(jnp.bfloat16)
+    context_ref[:, 256:] = sums[1][:, 128:].astype(jnp.bfloat16)
+    turned = jnp.dot(turn_ref[...], context_ref[...], preferred_element_type=jnp.float32)
+    out_ref[...] = turned.astype(jnp.bfloat16)
+
+
+def encoder_attention(q, kv, offset, turn):
     return pl.pallas_call(
         encoder_kernel,
-        in_specs=[pl.BlockSpec(memory_space=pltpu.VMEM)] * 3,
+        in_specs=[pl.BlockSpec(memory_space=pltpu.VMEM)] * 4,
         out_specs=pl.BlockSpec(memory_space=pltpu.VMEM),
         out_shape=jax.ShapeDtypeStruct(q.shape, jnp.bfloat16),
+        scratch_shapes=[pltpu.VMEM(q.shape, jnp.bfloat16)],
         cost_estimate=pl.CostEstimate(flops=9 * 10**9, bytes_accessed=5 * 10**6, transcendentals=5 * 10**6),
         name="encoder_attention",
-    )(q, kv, offset)
+    )(q, kv, offset, turn)
+
+
+MESH = pl.DeviceIdType.MESH
+
+
+def finish_kernel(groups, context_ref, w_ref, tokens_ref, gain_ref, bias_ref, dec_ref, out_ref, got, send, recv):
+    seq, head = lax.axis_index("seq"), lax.axis_index("head")
+    barrier = pltpu.get_barrier_semaphore()
+    for step in range(1, groups):
+        peer = lax.rem(head + step, groups)
+        pl.semaphore_signal(barrier, inc=1, device_id=(seq, peer), device_id_type=MESH)
+    pl.semaphore_wait(barrier, groups - 1)
+    copies = []
+    for step in range(1, groups):
+        peer = lax.rem(head + step, groups)
+        copy = pltpu.make_async_remote_copy(
+            src_ref=context_ref.at[peer],
+            dst_ref=got.at[step - 1],
+            send_sem=send.at[step - 1],
+            recv_sem=recv.at[step - 1],
+            device_id=(seq, peer),
+            device_id_type=MESH,
+        )
+        copy.start()
+        copies.append(copy)
+    total = jnp.dot(context_ref[head], w_ref[head], preferred_element_type=jnp.float32)
+    for step in range(1, groups):
+        copies[step - 1].wait()
+        source = lax.rem(head + groups - step, groups)
+        total = total + jnp.dot(got[step - 1], w_ref[source], preferred_element_type=jnp.float32)
+    gain, bias = gain_ref[...].reshape(1, D), bias_ref[...].reshape(1, D)
+    rows = layer_norm(tokens_ref[...] + total, gain, bias).astype(jnp.bfloat16)
+    out_ref[...] = jnp.dot(rows, dec_ref[...], preferred_element_type=jnp.float32).astype(jnp.bfloat16)
+
+
+def finish_encoder(context, w, tokens, gain, bias, to_decoder):
+    groups, width = w.shape[0], w.shape[1]
+    return pl.pallas_call(
+        lambda *refs: finish_kernel(groups, *refs),
+        in_specs=[pl.BlockSpec(memory_space=pltpu.VMEM)] * 6,
+        out_specs=pl.BlockSpec(memory_space=pltpu.VMEM),
+        out_shape=jax.ShapeDtypeStruct((QUARTER, DD), jnp.bfloat16),
+        scratch_shapes=[
+            pltpu.VMEM((groups - 1, QUARTER, width), jnp.bfloat16),
+            pltpu.SemaphoreType.DMA((groups - 1,)),
+            pltpu.SemaphoreType.DMA((groups - 1,)),
+        ],
+        compiler_params=pltpu.CompilerParams(collective_id=0, has_side_effects=True),
+        cost_estimate=pl.CostEstimate(flops=5 * 10**8, bytes_accessed=6 * 10**6, transcendentals=0),
+        name="finish_encoder",
+    )(context.reshape(groups, QUARTER, width), w, tokens, gain, bias, to_decoder)
+
+
+def hand_over_kernel(count, groups, x_ref, out_ref, held, send, recv, spread_send, spread_recv):
+    seq, head = lax.axis_index("seq"), lax.axis_index("head")
+    barrier = pltpu.get_barrier_semaphore()
+
+    def greet(step, carry):
+        peer = lax.rem(seq + step, count)
+        pl.semaphore_signal(barrier, inc=1, device_id=(peer, head), device_id_type=MESH)
+        return carry
+
+    lax.fori_loop(1, count, greet, 0)
+    for step in range(1, groups):
+        peer = lax.rem(head + step, groups)
+        pl.semaphore_signal(barrier, inc=1, device_id=(seq, peer), device_id_type=MESH)
+    pl.semaphore_wait(barrier, count + groups - 2)
+
+    def copy_to(step):
+        peer = lax.rem(seq + step, count)
+        return pltpu.make_async_remote_copy(
+            src_ref=x_ref.at[peer],
+            dst_ref=held.at[head, seq],
+            send_sem=send.at[step],
+            recv_sem=recv.at[step],
+            device_id=(peer, head),
+            device_id_type=MESH,
+        )
+
+    def start(step, carry):
+        copy_to(step).start()
+        return carry
+
+    def finish(step, carry):
+        copy_to(step).wait()
+        return carry
+
+    lax.fori_loop(1, count, start, 0)
+    own = pltpu.make_async_copy(x_ref.at[seq], held.at[head, seq], send.at[0])
+    own.start()
+    own.wait()
+    lax.fori_loop(1, count, finish, 0)
+    copies = []
+    for step in range(1, groups):
+        peer = lax.rem(head + step, groups)
+        copy = pltpu.make_async_remote_copy(
+            src_ref=held.at[head],
+            dst_ref=held.at[head],
+            send_sem=spread_send.at[step - 1],
+            recv_sem=spread_recv.at[step - 1],
+            device_id=(seq, peer),
+            device_id_type=MESH,
+        )
+        copy.start()
+        copies.append(copy)
+    for copy in copies:
+        copy.wait()
+    out_ref[...] = held[...]
+
+
+def hand_over(x, groups):
+    count = x.shape[0]
+    shape = (groups, *x.shape)
+    return pl.pallas_call(
+        lambda *refs: hand_over_kernel(count, groups, *refs),
+        in_specs=[pl.BlockSpec(memory_space=pltpu.VMEM)],
+        out_specs=pl.BlockSpec(memory_space=pltpu.VMEM),
+        out_shape=jax.ShapeDtypeStruct(shape, jnp.bfloat16),
+        scratch_shapes=[
+            pltpu.VMEM(shape, jnp.bfloat16),
+            pltpu.SemaphoreType.DMA((count,)),
+            pltpu.SemaphoreType.DMA((count,)),
+            pltpu.SemaphoreType.DMA((groups - 1,)),
+            pltpu.SemaphoreType.DMA((groups - 1,)),
+        ],
+        compiler_params=pltpu.CompilerParams(collective_id=1, has_side_effects=True),
+        name="hand_over",
+    )(x)
 
 
 def body(
@@ -416,6 +554,8 @@
     offsets = jnp.repeat(offset_rows, OWNVIS, axis=1)
     wkv = jnp.concatenate([dec_qkv[1], dec_qkv[2]], axis=1)
     k_masked, v_masked = make_tables(mask_token, dec_gain, dec_bias, wkv, keep)
+    own_proj, _ = lax.optimization_barrier((enc_proj, k_masked))
+    all_proj = lax.all_gather(own_proj, "head")
 
     own_ids = jnp.arange(OWN, dtype=jnp.int32)
     own_frame, own_place = own_ids // BLOCK, own_ids % BLOCK
@@ -460,16 +600,13 @@
     vanishing = jnp.min(jnp.sum(base[2], axis=-1)) < 2.0**-60
     base = lax.cond(vanishing, by_clip, shared, None)
 
-    context = encoder_attention(enc_q, group_kv, jnp.where(live, 0.0, floor_score))
-    turned = jnp.dot(turn, context, preferred_element_type=jnp.float32).astype(jnp.bfloat16)
-    partial_out = jnp.dot(turned, enc_proj, preferred_element_type=jnp.float32).astype(jnp.bfloat16)
-    attended = lax.psum_scatter(partial_out, "head", scatter_dimension=0, tiled=True).astype(jnp.float32)
-    final_rows = layer_norm(tokens_part + attended, final_gain, final_bias).astype(jnp.bfloat16)
-    encoded = jnp.dot(final_rows, to_decoder, preferred_element_type=jnp.float32).astype(jnp.bfloat16)
-
-    arrived = lax.all_to_all(encoded.reshape(seq_count, VB, DD), "seq", split_axis=0, concat_axis=0, tiled=True)
-    arrived = lax.all_gather(arrived, "head")
-    a_ids = jnp.arange(4, dtype=jnp.int32)[:, None, None]
+    context = encoder_attention(enc_q, group_kv, jnp.where(live, 0.0, floor_score), turn)
+    encoded = finish_encoder(context, all_proj, tokens_part, final_gain, final_bias, to_decoder)
+
+    groups = all_proj.shape[0]
+    blocks = jnp.pad(encoded.reshape(seq_count, VB * DD // CHUNK, CHUNK), ((0, 0), (0, 4), (0, 0)))
+    arrived = hand_over(blocks, groups)[:, :, : VB * DD // CHUNK]
+    a_ids = jnp.arange(groups, dtype=jnp.int32)[:, None, None]
     from_ids = jnp.arange(seq_count, dtype=jnp.int32)
     i_ids = jnp.arange(VB, dtype=jnp.int32)[None, None, :]
     from_start = starts.T.reshape(-1)[None, :, None]

time: 242 us -> 242 us (level)
  Pallas kernels: 112 us -> 146 us
  local copies, waits for them, and re-layouts: 19.5 us -> 9.61 us
  blocking collectives: 9.86 us -> 0 us
  starting transfers between devices: 9.24 us -> 0.09 us
  matrix products: 10 us -> 4.09 us
  waiting for transfers between devices: 50.8 us -> 54 us
    all_gather x0 -> x1, waiting for transfers between devices: none -> 33.6 us  [body(): all_proj = lax.all_gather(own_proj, 'head')]
    pallas_call x0 -> x2, Pallas kernels: none -> 32.2 us  [the longest x1 21.7 us: hand_over(): pl.pallas_call(lambda *refs: hand_over_kernel(count, groups, *refs), in_s...]
    reduce_scatter x1 -> x0, waiting for transfers between devices: 19.6 us -> none  [body(): lax.psum_scatter(partial_out, 'head', scatter_dimension=0, tiled=True)]
    all_gather x1 -> x0, blocking collectives: 9.86 us -> none  [body(): arrived = lax.all_gather(arrived, 'head')]
    all_to_all x1 -> x0, starting transfers between devices: 9.16 us -> none  [body(): lax.all_to_all(encoded.reshape(seq_count, VB, DD), 'seq', split_axis=0, c...]
    all_to_all x1 -> x0, waiting for transfers between devices: 7.37 us -> none  [body(): lax.all_to_all(encoded.reshape(seq_count, VB, DD), 'seq', split_axis=0, c...]
    all_gather x2 -> x0, local copies, waits for them, and re-layouts: 6.86 us -> none  [the longest x1 6.52 us: body(): group_kv = lax.all_gather(enc_kv, 'seq', axis_index_groups=groups)]
    dot_general x2 -> x0, matrix products: 4.84 us -> none  [the longest x1 3.47 us: body(): jnp.dot(turned, enc_proj, preferred_element_type=jnp.float32)]
  transfers between devices with their start and end apart: 4 -> 3, of which waited for: 4 -> 3; matrix products, arithmetic and copies ran while one was open for 9% -> 9% of each run, Pallas kernels for 31% -> 36%
where the time goes in v2:
time: 242 us
  Pallas kernels  146 us (60%)
  waiting for transfers between devices  54 us (22%)
  between operations  14.3 us (6%)
  other arithmetic  14 us (6%)
  local copies, waits for them, and re-layouts  9.61 us (4%)
  matrix products  4.09 us (2%)
    pallas_call x1, Pallas kernels, base_attention(): pl.pallas_call(base_kernel, grid=(2, CHUNKS), in_specs=[pl.BlockSpec((1,...  35 us
    all_gather x1, waiting for transfers between devices, body(): all_proj = lax.all_gather(own_proj, 'head')  33.6 us
    pallas_call x1, Pallas kernels, make_tables(): pl.pallas_call(table_kernel, grid=(steps,), in_specs=[pl.BlockSpec((1, TI...  22.4 us
    pallas_call x1, Pallas kernels, hand_over(): pl.pallas_call(lambda *refs: hand_over_kernel(count, groups, *refs), in_s...  21.7 us
    pallas_call x1, Pallas kernels, join_attention(): pl.pallas_call(join_kernel, grid=(CLIPS,), in_specs=[pl.BlockSpec((2, OWN...  19.5 us
    all_gather x1, waiting for transfers between devices, body(): all_kv = lax.all_gather(vis_kv, 'seq')  18.2 us
    pallas_call x1, Pallas kernels, single_attention(): pl.pallas_call(single_kernel, grid=(blocks, CHUNKS), in_specs=[pl.BlockSp...  17.4 us
    pallas_call x1, Pallas kernels, encoder_attention(): pl.pallas_call(encoder_kernel, in_specs=[pl.BlockSpec(memory_space=pltpu....  13.1 us
  transfers between devices with their start and end apart: 3, of which 3 were waited for; matrix products, arithmetic and copies ran while one was open for 9% of the time, Pallas kernels for 36%

profile of v2, /device:TPU:1, one launch (start us, length us, event | category | flops | bytes accessed | tf_op | source)
XLA Modules:
  0.0 241.7 jit_solution(1092383733660223419)
XLA Ops:
  6.5 6.0 %encoder_projections.1 = (bf16[384,352]{1,0:T(8,128)(2,1)}, bf16[2,352,384]{2,1,0:T(8,128)(2,1)}) custom-call(bf16[384,1408]{1,0:T(8,128)(2,1)} %x_ref.1, f32[1408]{0:T(1024)} %gain_ref.1, f32[1408]{0:T(1024)} %bias_ref.1, bf16[3,352,1408]{2,1,0:T(8,128)(2,1)} %bitcast.111), custom_call_target="tpu_custom_call" | custom-call | flops 1200000000 | bytes 5000000 | tf_op jit(solution)/shard_map/encoder_projections/pallas_call | solution.py:316
  12.8 2.8 %multiply_sine_fusion = (f32[128,512]{1,0:T(8,128)}, f32[128,512]{1,0:T(8,128)}, f32[128,512]{1,0:T(8,128)}, f32[128,512]{1,0:T(8,128)}) fusion(f32[128]{0:T(128)S(1)} %iota_convert_fusion, f32[512]{0:T(512)S(1)} %fusion.41, f32[128]{0:T(128)S(1)} %convert_element_type.108, pred[512]{0:T(512)(128)(4,1)S(1)} %fusion.36), kind=kLoop, calls=%fused_computation.35 | loop fusion | flops 327680 | bytes 1052160 | tf_op jit(solution)/shard_map/sin | solution.py:81
  15.7 0.7 pad_maximum_fusion.wkv
  16.7 1.7 fusion.29
  18.5 22.4 %masked_tables.1 = (bf16[16384,128]{1,0:T(8,128)(2,1)}, bf16[2,16384,256]{2,1,0:T(8,128)(2,1)}) custom-call(f32[16,8,512]{2,1,0:T(8,128)} %bitcast.101, f32[16,8,512]{2,1,0:T(8,128)} %bitcast.102, f32[128,512]{1,0:T(8,128)} %get-tuple-element.140.b1, f32[128,512]{1,0:T(8,128)} %get-tuple-element.141.b2, f32[1,512]{1,0:T(1,128)} %bitcast.104, ...), custom_call_target="tpu_custom_call" | custom-call | flops 20000000000 | bytes 25000000 | tf_op jit(solution)/shard_map/masked_tables/pallas_call | solution.py:91
  41.0 0.7 broadcast_subtract_fusion
  43.3 0.7 add_select_fusion.4
  44.5 0.6 copy.44
  48.4 0.9 fusion.31
  49.5 1.1 fusion.16.refs_2_
  50.6 35.0 %masked_queries.1 = (f32[2,512,256]{2,1,0:T(8,128)}, f32[2,512,128]{2,1,0:T(8,128)}, f32[2,4,512,128]{3,2,1,0:T(8,128)}) custom-call(bf16[2,512,128]{2,1,0:T(8,128)(2,1)S(1)} %broadcast_select_fusion.q_ref.qb_ref, bf16[16384,128]{1,0:T(8,128)(2,1)} %get-tuple-element.142.k_ref, bf16[2,16384,256]{2,1,0:T(8,128)(2,1)} %get-tuple-element.143.v_ref, ...), custom_call_target="tpu_custom_call" | custom-call | flops 24999999488 | bytes 25000000 | tf_op jit(solution)/shard_map/masked_queries/pallas_call | solution.py:154
  85.6 2.2 all-gather.8.cloned.1.call-done
  87.8 13.1 %encoder_attention.1 = bf16[384,352]{1,0:T(8,128)(2,1)} custom-call(bf16[384,352]{1,0:T(8,128)(2,1)} %get-tuple-element.148.q_ref, bf16[8,2,352,384]{3,2,1,0:T(8,128)(2,1)} %bitcast.110, f32[1,3072]{1,0:T(1,128)} %bitcast.106, bf16[384,384]{1,0:T(8,128)(2,1)} %get-tuple-element.150.turn_ref), custom_call_target="tpu_custom_call" | custom-call | flops 8999999488 | bytes 5000000 | tf_op jit(solution)/shard_map/encoder_attention/pallas_call | solution.py:376
  100.9 33.6 %all-gather.10.cloned.1.call-done = bf16[1408,1408]{1,0:T(8,128)(2,1)} async-done(((bf16[352,1408]{1,0:T(8,128)(2,1)}), bf16[1408,1408]{1,0:T(8,128)(2,1)}) %all-gather.10.cloned.1.call-update) | async-done | bytes 3964944 | tf_op jit(solution)/shard_map/all_gather | solution.py:558
  134.5 10.5 %finish_encoder.1 = bf16[96,512]{1,0:T(8,128)(2,1)} custom-call(bf16[4,96,352]{2,1,0:T(8,128)(2,1)} %bitcast.100, bf16[4,352,1408]{2,1,0:T(8,128)(2,1)} %bitcast.90, f32[96,1408]{1,0:T(8,128)} %fusion.16.refs_2_, f32[1408]{0:T(1024)} %refs_3_.1, f32[1408]{0:T(1024)} %refs_4_.1, bf16[1408,512]{1,0:T(8,128)(2,1)} %refs_5_.1), custom_call_target="tpu_custom_call" | custom-call | flops 500000000 | bytes 6000000 | tf_op jit(solution)/shard_map/finish_encoder/pallas_call | solution.py:422
  144.9 1.0 reshape.613
  145.9 0.7 pad.4.refs_0_
  146.6 21.7 %hand_over.1 = bf16[4,32,16,128]{3,2,1,0:T(8,128)(2,1)} custom-call(bf16[32,16,128]{2,1,0:T(8,128)(2,1)} %pad.4.refs_0_), custom_call_target="tpu_custom_call" | custom-call | tf_op jit(solution)/shard_map/hand_over/pallas_call | solution.py:498
  168.3 1.4 reshape.614
  171.1 0.6 pad_maximum_fusion.1
  171.8 0.7 broadcast_in_dim.224
  172.8 1.2 and_convert_fusion.place_ref
  174.0 0.6 reduce_sum.49
  174.6 0.7 reduce_min.9
  176.0 1.6 conditional.1
  176.0 1.6 broadcast_in_dim.108.clone
  177.8 0.7 broadcast_select_fusion.1.q_ref
  178.4 0.6 broadcast_select_fusion.2.qv_ref
  179.1 0.9 broadcast_in_dim.223
  180.0 17.4 %visible_queries.1 = (f32[2,192,256]{2,1,0:T(8,128)}, f32[2,192,128]{2,1,0:T(8,128)}, f32[2,192,128]{2,1,0:T(8,128)}) custom-call(bf16[2,192,128]{2,1,0:T(8,128)(2,1)} %broadcast_select_fusion.1.q_ref, bf16[16384,128]{1,0:T(8,128)(2,1)} %get-tuple-element.142.k_ref, bf16[2,16384,256]{2,1,0:T(8,128)(2,1)} %get-tuple-element.143.v_ref, f32[8,192,128]{2,1,0:T(8,128)} %bitcast.98), custom_call_target="tpu_custom_call" | custom-call | flops 20000000000 | bytes 25000000 | tf_op jit(solution)/shard_map/visible_queries/pallas_call | solution.py:203
  197.5 18.2 %all-gather.6.cloned.1.call-done.kv_ref = bf16[32,4,48,256]{3,2,1,0:T(8,128)(2,1)} async-done(((bf16[1,4,48,256]{3,2,1,0:T(8,128)(2,1)}), bf16[32,4,48,256]{3,2,1,0:T(8,128)(2,1)}) %all-gather.6.cloned.1.call-update) | async-done | bytes 3145744 | tf_op jit(solution)/shard_map/all_gather | solution.py:627
  215.7 19.5 %join_visible_keys.1 = bf16[4,512,128]{2,1,0:T(8,128)(2,1)} custom-call(bf16[2,512,128]{2,1,0:T(8,128)(2,1)S(1)} %broadcast_select_fusion.q_ref.qb_ref, bf16[2,4,48,128]{3,2,1,0:T(8,128)(2,1)} %broadcast_select_fusion.2.qv_ref, bf16[32,4,48,256]{3,2,1,0:T(8,128)(2,1)} %all-gather.6.cloned.1.call-done.kv_ref, f32[2,512,256]{2,1,0:T(8,128)} %get-tuple-element.156.accb_ref, ...), custom_call_target="tpu_custom_call" | custom-call | flops 8000000000 | bytes 10000000 | tf_op jit(solution)/shard_map/join_visible_keys/pallas_call | solution.py:275
  (101 shorter events, 7.9 us)
Async XLA Ops:
  6.5 81.2 %all-gather.8.cloned.1.call-start = ((), (), s32[]{:S(2)}) async-start(), calls=%async_computation.1 | async-start | bytes 4866048 | tf_op jit(solution)/shard_map/all_gather | solution.py:543
  6.5 9.1 %copy-start.4 = (bf16[3,512,128]{2,1,0:T(8,128)(2,1)S(1)}, bf16[3,512,128]{2,1,0:T(8,128)(2,1)}, u32[]{:S(2)}) copy-start(bf16[3,512,128]{2,1,0:T(8,128)(2,1)} %param.31) | copy-start | bytes 1179652
  12.5 3.9 %copy-start.11 = (s32[4,96]{1,0:T(4,128)S(1)}, s32[4,96]{1,0:T(4,128)}, u32[]{:S(2)}) copy-start(s32[4,96]{1,0:T(4,128)} %param.20) | copy-start | bytes 4612
  12.6 121.9 %all-gather.10.cloned.1.call-start = ((), (), s32[]{:S(2)}) async-start(), calls=%async_computation.2 | async-start | bytes 4956160 | tf_op jit(solution)/shard_map/all_gather | solution.py:558
  18.5 24.1 %copy-start.8 = (s32[4,8]{1,0:T(4,128)S(1)}, s32[4,8]{1,0:T(4,128)}, u32[]{:S(2)}) copy-start(s32[4,8]{1,0:T(4,128)} %param.19) | copy-start | bytes 388
  18.5 25.7 %copy-start.7 = (f32[512]{0:T(512)S(1)}, f32[512]{0:T(512)}, u32[]{:S(2)}) copy-start(f32[512]{0:T(512)} %param.28) | copy-start | bytes 6148
  40.9 6.9 %copy-start.9 = (f32[512]{0:T(512)S(1)}, f32[512]{0:T(512)}, u32[]{:S(2)}) copy-start(f32[512]{0:T(512)} %param.30) | copy-start | bytes 6148
  40.9 6.9 %copy-start.10 = (f32[512]{0:T(512)S(1)}, f32[512]{0:T(512)}, u32[]{:S(2)}) copy-start(f32[512]{0:T(512)} %param.29) | copy-start | bytes 6148
  40.9 174.8 %all-gather.6.cloned.1.call-start = ((), (), s32[]{:S(2)}) async-start(), calls=%async_computation | async-start | bytes 3244032 | tf_op jit(solution)/shard_map/all_gather | solution.py:627
  44.4 5.0 %copy-start.5 = (bf16[384,1408]{1,0:T(8,128)(2,1)S(1)}, bf16[384,1408]{1,0:T(8,128)(2,1)}, u32[]{:S(2)}) copy-start(bf16[384,1408]{1,0:T(8,128)(2,1)} %x_ref.1) | copy-start | bytes 3244036
  47.1 1.3 copy-start.12
  169.9 4.1 %copy-start.1 = (f32[2,4,512,128]{3,2,1,0:T(8,128)S(1)}, f32[2,4,512,128]{3,2,1,0:T(8,128)}, u32[]{:S(2)}) copy-start(f32[2,4,512,128]{3,2,1,0:T(8,128)} %get-tuple-element.153) | copy-start | bytes 6291460
  170.9 5.1 %copy-start.6 = (f32[2,512,128]{2,1,0:T(8,128)S(1)}, f32[2,512,128]{2,1,0:T(8,128)}, u32[]{:S(2)}) copy-start(f32[2,512,128]{2,1,0:T(8,128)} %get-tuple-element.154) | copy-start | bytes 1572868
  176.0 1.8 copy-start.13
Sparse Core Ops, SparseCore 0:
  12.7 75.0 all-gather.7
  89.4 44.9 all-gather.9
  171.9 43.7 all-gather.5

commit v3 on v2

--- a/solution.py
+++ b/solution.py
@@ -124,6 +124,7 @@
 
 BASE_ROWS = 128
 JOIN_ROWS = 512
+SLOW_ROWS = 32
 
 
 def base_kernel(q_ref, k_ref, v_ref, keep_ref, acc_ref, m_ref, l_ref):
@@ -336,7 +337,7 @@
     )(x, gain, bias, w)
 
 
-def encoder_kernel(q_ref, kv_ref, offset_ref, turn_ref, out_ref, context_ref):
+def encoder_kernel(q_ref, kv_ref, offset_ref, turn_ref, proj_ref, out_ref, context_ref):
     width = q_ref.shape[1]
     head_size = D // HEADS
     scale = LOG2E / math.sqrt(head_size)
@@ -369,25 +370,26 @@
     context_ref[:, 128:256] = (sums[0][:, 128:] + sums[1][:, :128]).astype(jnp.bfloat16)
     context_ref[:, 256:] = sums[1][:, 128:].astype(jnp.bfloat16)
     turned = jnp.dot(turn_ref[...], context_ref[...], preferred_element_type=jnp.float32)
-    out_ref[...] = turned.astype(jnp.bfloat16)
-
-
-def encoder_attention(q, kv, offset, turn):
+    turned = turned.astype(jnp.bfloat16)
+    out_ref[...] = jnp.dot(turned, proj_ref[...], preferred_element_type=jnp.float32).astype(jnp.bfloat16)
+
+
+def encoder_attention(q, kv, offset, turn, proj):
     return pl.pallas_call(
         encoder_kernel,
-        in_specs=[pl.BlockSpec(memory_space=pltpu.VMEM)] * 4,
+        in_specs=[pl.BlockSpec(memory_space=pltpu.VMEM)] * 5,
         out_specs=pl.BlockSpec(memory_space=pltpu.VMEM),
-        out_shape=jax.ShapeDtypeStruct(q.shape, jnp.bfloat16),
+        out_shape=jax.ShapeDtypeStruct((q.shape[0], D), jnp.bfloat16),
         scratch_shapes=[pltpu.VMEM(q.shape, jnp.bfloat16)],
         cost_estimate=pl.CostEstimate(flops=9 * 10**9, bytes_accessed=5 * 10**6, transcendentals=5 * 10**6),
         name="encoder_attention",
-    )(q, kv, offset, turn)
+    )(q, kv, offset, turn, proj)
 
 
 MESH = pl.DeviceIdType.MESH
 
 
-def finish_kernel(groups, context_ref, w_ref, tokens_ref, gain_ref, bias_ref, dec_ref, out_ref, got, send, recv):
+def finish_kernel(groups, parts_ref, tokens_ref, gain_ref, bias_ref, dec_ref, out_ref, got, send, recv):
     seq, head = lax.axis_index("seq"), lax.axis_index("head")
     barrier = pltpu.get_barrier_semaphore()
     for step in range(1, groups):
@@ -398,7 +400,7 @@
     for step in range(1, groups):
         peer = lax.rem(head + step, groups)
         copy = pltpu.make_async_remote_copy(
-            src_ref=context_ref.at[peer],
+            src_ref=parts_ref.at[peer],
             dst_ref=got.at[step - 1],
             send_sem=send.at[step - 1],
             recv_sem=recv.at[step - 1],
@@ -407,32 +409,31 @@
         )
         copy.start()
         copies.append(copy)
-    total = jnp.dot(context_ref[head], w_ref[head], preferred_element_type=jnp.float32)
+    total = tokens_ref[...] + parts_ref[head].astype(jnp.float32)
     for step in range(1, groups):
         copies[step - 1].wait()
-        source = lax.rem(head + groups - step, groups)
-        total = total + jnp.dot(got[step - 1], w_ref[source], preferred_element_type=jnp.float32)
+        total = total + got[step - 1].astype(jnp.float32)
     gain, bias = gain_ref[...].reshape(1, D), bias_ref[...].reshape(1, D)
-    rows = layer_norm(tokens_ref[...] + total, gain, bias).astype(jnp.bfloat16)
+    rows = layer_norm(total, gain, bias).astype(jnp.bfloat16)
     out_ref[...] = jnp.dot(rows, dec_ref[...], preferred_element_type=jnp.float32).astype(jnp.bfloat16)
 
 
-def finish_encoder(context, w, tokens, gain, bias, to_decoder):
-    groups, width = w.shape[0], w.shape[1]
+def finish_encoder(parts, tokens, gain, bias, to_decoder):
+    groups = parts.shape[0] // QUARTER
     return pl.pallas_call(
         lambda *refs: finish_kernel(groups, *refs),
-        in_specs=[pl.BlockSpec(memory_space=pltpu.VMEM)] * 6,
+        in_specs=[pl.BlockSpec(memory_space=pltpu.VMEM)] * 5,
         out_specs=pl.BlockSpec(memory_space=pltpu.VMEM),
         out_shape=jax.ShapeDtypeStruct((QUARTER, DD), jnp.bfloat16),
         scratch_shapes=[
-            pltpu.VMEM((groups - 1, QUARTER, width), jnp.bfloat16),
+            pltpu.VMEM((groups - 1, QUARTER, D), jnp.bfloat16),
             pltpu.SemaphoreType.DMA((groups - 1,)),
             pltpu.SemaphoreType.DMA((groups - 1,)),
         ],
         compiler_params=pltpu.CompilerParams(collective_id=0, has_side_effects=True),
-        cost_estimate=pl.CostEstimate(flops=5 * 10**8, bytes_accessed=6 * 10**6, transcendentals=0),
+        cost_estimate=pl.CostEstimate(flops=2 * 10**8, bytes_accessed=3 * 10**6, transcendentals=0),
         name="finish_encoder",
-    )(context.reshape(groups, QUARTER, width), w, tokens, gain, bias, to_decoder)
+    )(parts.reshape(groups, QUARTER, D), tokens, gain, bias, to_decoder)
 
 
 def hand_over_kernel(count, groups, x_ref, out_ref, held, send, recv, spread_send, spread_recv):
@@ -554,8 +555,6 @@
     offsets = jnp.repeat(offset_rows, OWNVIS, axis=1)
     wkv = jnp.concatenate([dec_qkv[1], dec_qkv[2]], axis=1)
     k_masked, v_masked = make_tables(mask_token, dec_gain, dec_bias, wkv, keep)
-    own_proj, _ = lax.optimization_barrier((enc_proj, k_masked))
-    all_proj = lax.all_gather(own_proj, "head")
 
     own_ids = jnp.arange(OWN, dtype=jnp.int32)
     own_frame, own_place = own_ids // BLOCK, own_ids % BLOCK
@@ -586,9 +585,9 @@
 
     def by_clip(_):
         offset = jnp.broadcast_to(
-            offset_rows.transpose(1, 0, 2)[:, :, None, :], (CLIPS, CHUNKS, BASE_ROWS, CHUNK)
+            offset_rows.transpose(1, 0, 2)[:, :, None, :], (CLIPS, CHUNKS, SLOW_ROWS, CHUNK)
         )
-        accs, ms, ls = lax.map(lambda x: single_attention(q_masked, k_masked, v_masked, x, BASE_ROWS), offset)
+        accs, ms, ls = lax.map(lambda x: single_attention(q_masked, k_masked, v_masked, x, SLOW_ROWS), offset)
         acc = accs[0]
         for clip in range(1, CLIPS):
             acc = jnp.where(lane_clip[None, None, :] == clip, accs[clip], acc)
@@ -600,10 +599,10 @@
     vanishing = jnp.min(jnp.sum(base[2], axis=-1)) < 2.0**-60
     base = lax.cond(vanishing, by_clip, shared, None)
 
-    context = encoder_attention(enc_q, group_kv, jnp.where(live, 0.0, floor_score), turn)
-    encoded = finish_encoder(context, all_proj, tokens_part, final_gain, final_bias, to_decoder)
-
-    groups = all_proj.shape[0]
+    parts = encoder_attention(enc_q, group_kv, jnp.where(live, 0.0, floor_score), turn, enc_proj)
+    encoded = finish_encoder(parts, tokens_part, final_gain, final_bias, to_decoder)
+
+    groups = lax.axis_size("head")
     blocks = jnp.pad(encoded.reshape(seq_count, VB * DD // CHUNK, CHUNK), ((0, 0), (0, 4), (0, 0)))
     arrived = hand_over(blocks, groups)[:, :, : VB * DD // CHUNK]
     a_ids = jnp.arange(groups, dtype=jnp.int32)[:, None, None]

time: 242 us -> 217 us (0.90)
  waiting for transfers between devices: 54 us -> 21.5 us
  Pallas kernels: 146 us -> 154 us
    all_gather x1 -> x0, waiting for transfers between devices: 33.6 us -> none  [body(): all_proj = lax.all_gather(own_proj, 'head')]
    pallas_call x1, Pallas kernels: 10.5 us -> 18 us  [finish_encoder(): pl.pallas_call(lambda *refs: finish_kernel(groups, *refs), in_specs=[pl.B...]
  transfers between devices with their start and end apart: 3 -> 2, of which waited for: 3 -> 2; matrix products, arithmetic and copies ran while one was open for 9% -> 10% of each run, Pallas kernels for 36% -> 35%
where the time goes in v3:
time: 217 us
  Pallas kernels  154 us (71%)
  waiting for transfers between devices  21.5 us (10%)
  other arithmetic  14.9 us (7%)
  between operations  14.5 us (7%)
  local copies, waits for them, and re-layouts  7.8 us (4%)
  matrix products  4.08 us (2%)
    pallas_call x1, Pallas kernels, base_attention(): pl.pallas_call(base_kernel, grid=(2, CHUNKS), in_specs=[pl.BlockSpec((1,...  35 us
    pallas_call x1, Pallas kernels, make_tables(): pl.pallas_call(table_kernel, grid=(steps,), in_specs=[pl.BlockSpec((1, TI...  22.4 us
    pallas_call x1, Pallas kernels, hand_over(): pl.pallas_call(lambda *refs: hand_over_kernel(count, groups, *refs), in_s...  21.2 us
    pallas_call x1, Pallas kernels, join_attention(): pl.pallas_call(join_kernel, grid=(CLIPS,), in_specs=[pl.BlockSpec((2, OWN...  19.5 us
    all_gather x1, waiting for transfers between devices, body(): all_kv = lax.all_gather(vis_kv, 'seq')  18.5 us
    pallas_call x1, Pallas kernels, finish_encoder(): pl.pallas_call(lambda *refs: finish_kernel(groups, *refs), in_specs=[pl.B...  18 us
    pallas_call x1, Pallas kernels, single_attention(): pl.pallas_call(single_kernel, grid=(blocks, CHUNKS), in_specs=[pl.BlockSp...  17.5 us
    pallas_call x1, Pallas kernels, encoder_attention(): pl.pallas_call(encoder_kernel, in_specs=[pl.BlockSpec(memory_space=pltpu....  14.4 us
  transfers between devices with their start and end apart: 2, of which 2 were waited for; matrix products, arithmetic and copies ran while one was open for 10% of the time, Pallas kernels for 35%

profile of v3, /device:TPU:1, one launch (start us, length us, event | category | flops | bytes accessed | tf_op | source)
XLA Modules:
  0.0 216.7 jit_solution(4840341147381542565)
XLA Ops:
  6.5 5.9 %encoder_projections.1 = (bf16[384,352]{1,0:T(8,128)(2,1)}, bf16[2,352,384]{2,1,0:T(8,128)(2,1)}) custom-call(bf16[384,1408]{1,0:T(8,128)(2,1)} %x_ref.1, f32[1408]{0:T(1024)} %gain_ref.1, f32[1408]{0:T(1024)} %bias_ref.1, bf16[3,352,1408]{2,1,0:T(8,128)(2,1)} %bitcast.109), custom_call_target="tpu_custom_call" | custom-call | flops 1200000000 | bytes 5000000 | tf_op jit(solution)/shard_map/encoder_projections/pallas_call | solution.py:317
  12.9 0.4 multiply_sine_fusion.2
  13.8 2.8 %multiply_sine_fusion = (f32[128,512]{1,0:T(8,128)}, f32[128,512]{1,0:T(8,128)}, f32[128,512]{1,0:T(8,128)}, f32[128,512]{1,0:T(8,128)}) fusion(f32[128]{0:T(128)S(1)} %iota_convert_fusion, f32[512]{0:T(512)S(1)} %fusion.41, f32[128]{0:T(128)S(1)} %convert_element_type.108, pred[512]{0:T(512)(128)(4,1)S(1)} %fusion.36), kind=kLoop, calls=%fused_computation.35 | loop fusion | flops 327680 | bytes 1052160 | tf_op jit(solution)/shard_map/sin | solution.py:81
  16.9 0.6 dynamic_slice.18
  17.5 0.6 add_select_fusion.4
  18.2 0.6 copy.44
  20.5 0.7 pad_maximum_fusion.wkv
  21.9 0.4 multiply_reduce_fusion
  22.3 0.6 select_bitcast_fusion.keep_ref
  23.6 0.9 fusion.31
  24.6 1.7 fusion.29
  26.3 1.1 fusion.16.refs_1_
  27.5 22.4 %masked_tables.1 = (bf16[16384,128]{1,0:T(8,128)(2,1)}, bf16[2,16384,256]{2,1,0:T(8,128)(2,1)}) custom-call(f32[16,8,512]{2,1,0:T(8,128)} %bitcast.99, f32[16,8,512]{2,1,0:T(8,128)} %bitcast.100, f32[128,512]{1,0:T(8,128)} %get-tuple-element.139.b1, f32[128,512]{1,0:T(8,128)} %get-tuple-element.140.b2, f32[1,512]{1,0:T(1,128)} %bitcast.102, ...), custom_call_target="tpu_custom_call" | custom-call | flops 20000000000 | bytes 25000000 | tf_op jit(solution)/shard_map/masked_tables/pallas_call | solution.py:91
  49.8 35.0 %masked_queries.1 = (f32[2,512,256]{2,1,0:T(8,128)}, f32[2,512,128]{2,1,0:T(8,128)S(1)}, f32[2,4,512,128]{3,2,1,0:T(8,128)}) custom-call(bf16[2,512,128]{2,1,0:T(8,128)(2,1)S(1)} %broadcast_select_fusion.q_ref.qb_ref, bf16[16384,128]{1,0:T(8,128)(2,1)} %get-tuple-element.141.k_ref, bf16[2,16384,256]{2,1,0:T(8,128)(2,1)} %get-tuple-element.142.v_ref, ...), custom_call_target="tpu_custom_call" | custom-call | flops 24999999488 | bytes 25000000 | tf_op jit(solution)/shard_map/masked_queries/pallas_call | solution.py:155
  84.8 3.0 %all-gather.6.cloned.1.call-done = bf16[16,352,384]{2,1,0:T(8,128)(2,1)} async-done(((bf16[2,352,384]{2,1,0:T(8,128)(2,1)}), bf16[16,352,384]{2,1,0:T(8,128)(2,1)}) %all-gather.6.cloned.1.call-update) | async-done | bytes 4325392 | tf_op jit(solution)/shard_map/all_gather | solution.py:544
  87.8 14.4 %encoder_attention.1 = bf16[384,1408]{1,0:T(8,128)(2,1)} custom-call(bf16[384,352]{1,0:T(8,128)(2,1)} %get-tuple-element.147.q_ref, bf16[8,2,352,384]{3,2,1,0:T(8,128)(2,1)} %bitcast.108, f32[1,3072]{1,0:T(1,128)} %bitcast.104, bf16[384,384]{1,0:T(8,128)(2,1)} %get-tuple-element.149.turn_ref, bf16[352,1408]{1,0:T(8,128)(2,1)} %proj_ref.1), custom_call_target="tpu_custom_call" | custom-call | flops 8999999488 | bytes 5000000 | tf_op jit(solution)/shard_map/encoder_attention/pallas_call | solution.py:378
  102.2 18.0 %finish_encoder.1 = bf16[96,512]{1,0:T(8,128)(2,1)} custom-call(bf16[4,96,1408]{2,1,0:T(8,128)(2,1)} %bitcast.95, f32[96,1408]{1,0:T(8,128)} %fusion.16.refs_1_, f32[1408]{0:T(1024)} %refs_2_.1, f32[1408]{0:T(1024)} %refs_3_.1, bf16[1408,512]{1,0:T(8,128)(2,1)} %refs_4_.1), custom_call_target="tpu_custom_call" | custom-call | flops 200000000 | bytes 3000000 | tf_op jit(solution)/shard_map/finish_encoder/pallas_call | solution.py:423
  120.2 1.0 reshape.613
  121.2 0.7 pad.4.refs_0_
  121.9 21.2 %hand_over.1 = bf16[4,32,16,128]{3,2,1,0:T(8,128)(2,1)} custom-call(bf16[32,16,128]{2,1,0:T(8,128)(2,1)} %pad.4.refs_0_), custom_call_target="tpu_custom_call" | custom-call | tf_op jit(solution)/shard_map/hand_over/pallas_call | solution.py:499
  143.2 1.4 reshape.614
  144.8 0.4 fusion.57
  145.9 0.7 pad_maximum_fusion.1
  146.9 1.2 and_convert_fusion.place_ref
  148.1 2.2 %reduce_sum.49 = f32[2,4,512]{2,1,0:T(4,128)S(1)} reduce(f32[2,4,512,128]{3,2,1,0:T(8,128)} %get-tuple-element.151, f32[]{:T(128)} %constant.222.clone.1), dimensions={3}, to_apply=%region_6.7 | reduce | flops 520192 | bytes 2113540 | tf_op jit(solution)/shard_map/reduce_sum | solution.py:599
  150.3 0.6 reduce_min.9
  152.2 0.7 broadcast_select_fusion.1.q_ref
  152.9 0.6 broadcast_select_fusion.2.qv_ref
  153.5 0.9 broadcast_in_dim.223
  154.5 17.5 %visible_queries.1 = (f32[2,192,256]{2,1,0:T(8,128)}, f32[2,192,128]{2,1,0:T(8,128)}, f32[2,192,128]{2,1,0:T(8,128)}) custom-call(bf16[2,192,128]{2,1,0:T(8,128)(2,1)} %broadcast_select_fusion.1.q_ref, bf16[16384,128]{1,0:T(8,128)(2,1)} %get-tuple-element.141.k_ref, bf16[2,16384,256]{2,1,0:T(8,128)(2,1)} %get-tuple-element.142.v_ref, f32[8,192,128]{2,1,0:T(8,128)} %bitcast.97), custom_call_target="tpu_custom_call" | custom-call | flops 20000000000 | bytes 25000000 | tf_op jit(solution)/shard_map/visible_queries/pallas_call | solution.py:204
  171.9 18.5 %all-gather.4.cloned.1.call-done.kv_ref = bf16[32,4,48,256]{3,2,1,0:T(8,128)(2,1)} async-done(((bf16[1,4,48,256]{3,2,1,0:T(8,128)(2,1)}), bf16[32,4,48,256]{3,2,1,0:T(8,128)(2,1)}) %all-gather.4.cloned.1.call-update) | async-done | bytes 3145744 | tf_op jit(solution)/shard_map/all_gather | solution.py:626
  190.4 19.5 %join_visible_keys.1 = bf16[4,512,128]{2,1,0:T(8,128)(2,1)} custom-call(bf16[2,512,128]{2,1,0:T(8,128)(2,1)S(1)} %broadcast_select_fusion.q_ref.qb_ref, bf16[2,4,48,128]{3,2,1,0:T(8,128)(2,1)} %broadcast_select_fusion.2.qv_ref, bf16[32,4,48,256]{3,2,1,0:T(8,128)(2,1)} %all-gather.4.cloned.1.call-done.kv_ref, f32[2,512,256]{2,1,0:T(8,128)} %get-tuple-element.154.accb_ref, ...), custom_call_target="tpu_custom_call" | custom-call | flops 8000000000 | bytes 10000000 | tf_op jit(solution)/shard_map/join_visible_keys/pallas_call | solution.py:276
  (98 shorter events, 6.2 us)
Async XLA Ops:
  6.5 81.3 %all-gather.6.cloned.1.call-start = ((), (), s32[]{:S(2)}) async-start(), calls=%async_computation.1 | async-start | bytes 4866048 | tf_op jit(solution)/shard_map/all_gather | solution.py:544
  6.5 6.1 %copy-start.11 = (s32[4,96]{1,0:T(4,128)S(1)}, s32[4,96]{1,0:T(4,128)}, u32[]{:S(2)}) copy-start(s32[4,96]{1,0:T(4,128)} %param.20) | copy-start | bytes 4612
  12.5 4.2 %copy-start.3 = (bf16[3,512,128]{2,1,0:T(8,128)(2,1)S(1)}, bf16[3,512,128]{2,1,0:T(8,128)(2,1)}, u32[]{:S(2)}) copy-start(bf16[3,512,128]{2,1,0:T(8,128)(2,1)} %param.31) | copy-start | bytes 1179652
  12.5 4.3 %copy-start.6 = (s32[4,8]{1,0:T(4,128)S(1)}, s32[4,8]{1,0:T(4,128)}, u32[]{:S(2)}) copy-start(s32[4,8]{1,0:T(4,128)} %param.19) | copy-start | bytes 388
  12.5 9.1 %copy-start.5 = (f32[512]{0:T(512)S(1)}, f32[512]{0:T(512)}, u32[]{:S(2)}) copy-start(f32[512]{0:T(512)} %param.28) | copy-start | bytes 6148
  12.5 177.9 %all-gather.4.cloned.1.call-start = ((), (), s32[]{:S(2)}) async-start(), calls=%async_computation | async-start | bytes 3244032 | tf_op jit(solution)/shard_map/all_gather | solution.py:626
  12.9 10.0 %copy-start.7 = (f32[512]{0:T(512)S(1)}, f32[512]{0:T(512)}, u32[]{:S(2)}) copy-start(f32[512]{0:T(512)} %param.30) | copy-start | bytes 6148
  12.9 10.0 %copy-start.9 = (f32[512]{0:T(512)S(1)}, f32[512]{0:T(512)}, u32[]{:S(2)}) copy-start(f32[512]{0:T(512)} %param.29) | copy-start | bytes 6148
  22.2 4.1 %copy-start.4 = (bf16[384,1408]{1,0:T(8,128)(2,1)S(1)}, bf16[384,1408]{1,0:T(8,128)(2,1)}, u32[]{:S(2)}) copy-start(bf16[384,1408]{1,0:T(8,128)(2,1)} %x_ref.1) | copy-start | bytes 3244036
  22.3 1.4 copy-start.12
  121.9 23.4 %copy-start.8 = (f32[512]{0:T(512)S(1)}, f32[512]{0:T(512)}, u32[]{:S(2)}) copy-start(f32[512]{0:T(512)} %param.30) | copy-start | bytes 6148
  121.9 23.5 %copy-start.10 = (f32[512]{0:T(512)S(1)}, f32[512]{0:T(512)}, u32[]{:S(2)}) copy-start(f32[512]{0:T(512)} %param.29) | copy-start | bytes 6148
  151.6 0.6 copy-start.13
Sparse Core Ops, SparseCore 0:
  12.6 75.1 all-gather.5
  146.7 43.6 all-gather.3

commit v4 on v3

--- a/solution.py
+++ b/solution.py
@@ -53,22 +53,72 @@
     return jnp.where(even[None, :], jnp.sin(angles), jnp.cos(angles))
 
 
-TILES = 8
-
-
-def table_kernel(a1, a2, b1, b2, token, gain, bias, wkv, keep, k_ref, v_ref):
+TILES = 4
+
+
+def table_tile(tile, a1, a2, b1, b2, token, gain, bias, wkv, keep, k_ref, v_ref):
     lanes = lax.broadcasted_iota(jnp.int32, (1, 2 * HEAD), 1)
-    for tile in range(TILES):
-        rows = pl.ds(tile * CHUNK, CHUNK)
-        x = a1[0, tile : tile + 1, :] * b1[...] + a2[0, tile : tile + 1, :] * b2[...] + token[...]
-        h = layer_norm(x, gain[...], bias[...]).astype(jnp.bfloat16)
-        kv = jnp.dot(h, wkv[...], preferred_element_type=jnp.float32)
-        k_ref[rows, :] = kv[:, : 2 * HEAD].astype(jnp.bfloat16)
-        v = kv[:, 2 * HEAD :]
-        turned = pltpu.roll(v, HEAD, 1)
-        for head in range(2):
-            twice = jnp.where((lanes < HEAD) == (head == 0), v, turned)
-            v_ref[head, rows, :] = (jnp.concatenate([twice, twice], axis=1) * keep[0]).astype(jnp.bfloat16)
+    rows = pl.ds(pl.multiple_of(tile * CHUNK, CHUNK), CHUNK)
+    one = pl.ds(tile, 1)
+    x = a1[0, one, :] * b1[...] + a2[0, one, :] * b2[...] + token[...]
+    h = layer_norm(x, gain[...], bias[...]).astype(jnp.bfloat16)
+    kv = jnp.dot(h, wkv[...], preferred_element_type=jnp.float32)
+    k_ref[rows, :] = kv[:, : 2 * HEAD].astype(jnp.bfloat16)
+    v = kv[:, 2 * HEAD :]
+    turned = pltpu.roll(v, HEAD, 1)
+    for head in range(2):
+        twice = jnp.where((lanes < HEAD) == (head == 0), v, turned)
+        v_ref[head, rows, :] = (jnp.concatenate([twice, twice], axis=1) * keep[0]).astype(jnp.bfloat16)
+
+
+MESH = pl.DeviceIdType.MESH
+
+
+def masked_kernel(
+    a1, a2, b1, b2, token, gain, bias, wkv, keep, q_ref, keep_rows, kv_ref, k_ref, v_ref, acc_ref, m_ref, l_ref,
+    others_ref, send, recv,
+):
+    step = pl.program_id(0)
+    seq, head = lax.axis_index("seq"), lax.axis_index("head")
+    member, clip = seq // CLIPS, lax.rem(seq, CLIPS)
+
+    def peer(distance):
+        return (lax.rem(member + distance, GROUP) * CLIPS + clip, head)
+
+    def copy_to(distance):
+        return pltpu.make_async_remote_copy(
+            src_ref=kv_ref,
+            dst_ref=others_ref.at[distance - 1],
+            send_sem=send.at[distance - 1],
+            recv_sem=recv.at[distance - 1],
+            device_id=peer(distance),
+            device_id_type=MESH,
+        )
+
+    @pl.when(step == 0)
+    def _():
+        barrier = pltpu.get_barrier_semaphore()
+        for distance in range(1, GROUP):
+            pl.semaphore_signal(barrier, inc=1, device_id=peer(distance), device_id_type=MESH)
+        pl.semaphore_wait(barrier, GROUP - 1)
+        for distance in range(1, GROUP):
+            copy_to(distance).start()
+        acc_ref[...] = jnp.zeros_like(acc_ref)
+        l_ref[...] = jnp.zeros_like(l_ref)
+        m_ref[...] = jnp.full_like(m_ref, floor_score)
+
+    def tiles(part, carry):
+        for tile in range(TILES):
+            table_tile(part * TILES + tile, a1, a2, b1, b2, token, gain, bias, wkv, keep, k_ref, v_ref)
+        return carry
+
+    lax.fori_loop(0, FRAMES // TILES, tiles, 0)
+    base_chunk(q_ref, k_ref, v_ref, keep_rows, acc_ref, m_ref, l_ref)
+
+    @pl.when(step == CHUNKS - 1)
+    def _():
+        for distance in range(1, GROUP):
+            copy_to(distance).wait()
 
 
 def angle_tables(coarse, fine):
@@ -81,38 +131,49 @@
     return lax.optimization_barrier((a1, a2, jnp.cos(angle_b), jnp.sin(angle_b)))
 
 
-def make_tables(mask_token, dec_gain, dec_bias, wkv, keep):
+def masked_part(mask_token, dec_gain, dec_bias, wkv, keep, q, keep_rows, kv):
     coarse = (jnp.arange(FRAMES) * S)[None, :] + (jnp.arange(CHUNKS) * CHUNK)[:, None]
     a1, a2, b1, b2 = angle_tables(coarse.reshape(-1), jnp.arange(CHUNK))
-    a1, a2 = a1.reshape(-1, TILES, DD), a2.reshape(-1, TILES, DD)
-    steps = a1.shape[0]
-    per_chunk = steps // CHUNKS
+    a1, a2 = a1.reshape(CHUNKS, FRAMES, DD), a2.reshape(CHUNKS, FRAMES, DD)
     whole = lambda *shape: pl.BlockSpec(shape, lambda i: (0,) * len(shape))
     return pl.pallas_call(
-        table_kernel,
-        grid=(steps,),
+        masked_kernel,
+        grid=(CHUNKS,),
         in_specs=[
-            pl.BlockSpec((1, TILES, DD), lambda i: (i, 0, 0)),
-            pl.BlockSpec((1, TILES, DD), lambda i: (i, 0, 0)),
+            pl.BlockSpec((1, FRAMES, DD), lambda i: (i, 0, 0)),
+            pl.BlockSpec((1, FRAMES, DD), lambda i: (i, 0, 0)),
             whole(CHUNK, DD),
             whole(CHUNK, DD),
             whole(1, DD),
             whole(1, DD),
             whole(1, DD),
             whole(DD, 4 * HEAD),
-            pl.BlockSpec((1, CHUNK, CLIPS * HEAD), lambda i: (i // per_chunk, 0, 0)),
+            pl.BlockSpec((1, CHUNK, CLIPS * HEAD), lambda i: (i, 0, 0)),
+            whole(1, OWN, 2 * HEAD),
+            pl.BlockSpec((1, CLIPS, CHUNK), lambda i: (i, 0, 0)),
+            pl.BlockSpec(memory_space=pl.ANY),
         ],
         out_specs=[
-            pl.BlockSpec((TILES * CHUNK, 2 * HEAD), lambda i: (i, 0)),
-            pl.BlockSpec((2, TILES * CHUNK, CLIPS * HEAD), lambda i: (0, i, 0)),
+            pl.BlockSpec((KEYS, 2 * HEAD), lambda i: (i, 0)),
+            pl.BlockSpec((2, KEYS, CLIPS * HEAD), lambda i: (0, i, 0)),
+            whole(1, OWN, CLIPS * HEAD),
+            whole(1, OWN, CHUNK),
+            whole(1, CLIPS, OWN, CHUNK),
+            pl.BlockSpec(memory_space=pl.ANY),
         ],
         out_shape=[
             jax.ShapeDtypeStruct((L, 2 * HEAD), jnp.bfloat16),
             jax.ShapeDtypeStruct((2, L, CLIPS * HEAD), jnp.bfloat16),
-        ],
-        cost_estimate=pl.CostEstimate(flops=20 * 10**9, bytes_accessed=25 * 10**6, transcendentals=0),
-        name="masked_tables",
-    )(a1, a2, b1, b2, mask_token[None], dec_gain[None], dec_bias[None], wkv, keep)
+            jax.ShapeDtypeStruct((1, OWN, CLIPS * HEAD), jnp.float32),
+            jax.ShapeDtypeStruct((1, OWN, CHUNK), jnp.float32),
+            jax.ShapeDtypeStruct((1, CLIPS, OWN, CHUNK), jnp.float32),
+            jax.ShapeDtypeStruct((GROUP - 1, *kv.shape), jnp.bfloat16),
+        ],
+        scratch_shapes=[pltpu.SemaphoreType.DMA((GROUP - 1,)), pltpu.SemaphoreType.DMA((GROUP - 1,))],
+        compiler_params=pltpu.CompilerParams(collective_id=2, has_side_effects=True),
+        cost_estimate=pl.CostEstimate(flops=40 * 10**9, bytes_accessed=35 * 10**6, transcendentals=9 * 10**6),
+        name="masked_part",
+    )(a1, a2, b1, b2, mask_token[None], dec_gain[None], dec_bias[None], wkv, keep, q, keep_rows, kv)
 
 
 def lane_tiles(x):
@@ -123,19 +184,20 @@
 
 
 BASE_ROWS = 128
-JOIN_ROWS = 512
-SLOW_ROWS = 32
+SLOW_ROWS = 16
 
 
 def base_kernel(q_ref, k_ref, v_ref, keep_ref, acc_ref, m_ref, l_ref):
-    first = pl.program_id(1) == 0
-
-    @pl.when(first)
+    @pl.when(pl.program_id(0) == 0)
     def _():
         acc_ref[...] = jnp.zeros_like(acc_ref)
         l_ref[...] = jnp.zeros_like(l_ref)
         m_ref[...] = jnp.full_like(m_ref, floor_score)
 
+    base_chunk(q_ref, k_ref, v_ref, keep_ref, acc_ref, m_ref, l_ref)
+
+
+def base_chunk(q_ref, k_ref, v_ref, keep_ref, acc_ref, m_ref, l_ref):
     for start in range(0, OWN, BASE_ROWS):
         rows = pl.ds(start, BASE_ROWS)
         s = lax.dot_general(q_ref[0, rows, :], k_ref[...], NT, preferred_element_type=jnp.float32)
@@ -151,27 +213,27 @@
         acc_ref[0, rows, :] = acc_ref[0, rows, :] * jnp.concatenate([factor, factor], axis=1) + update
 
 
-def base_attention(q, k, v4, keep_rows):
+def base_attention(head, q, k, v4, keep_rows):
     return pl.pallas_call(
         base_kernel,
-        grid=(2, CHUNKS),
+        grid=(CHUNKS,),
         in_specs=[
-            pl.BlockSpec((1, OWN, 2 * HEAD), lambda h, j: (h, 0, 0)),
-            pl.BlockSpec((KEYS, 2 * HEAD), lambda h, j: (j, 0)),
-            pl.BlockSpec((1, KEYS, CLIPS * HEAD), lambda h, j: (h, j, 0)),
-            pl.BlockSpec((1, CLIPS, CHUNK), lambda h, j: (j, 0, 0)),
+            pl.BlockSpec((1, OWN, 2 * HEAD), lambda j: (0, 0, 0)),
+            pl.BlockSpec((KEYS, 2 * HEAD), lambda j: (j, 0)),
+            pl.BlockSpec((1, KEYS, CLIPS * HEAD), lambda j: (head, j, 0)),
+            pl.BlockSpec((1, CLIPS, CHUNK), lambda j: (j, 0, 0)),
         ],
         out_specs=[
-            pl.BlockSpec((1, OWN, CLIPS * HEAD), lambda h, j: (h, 0, 0)),
-            pl.BlockSpec((1, OWN, CHUNK), lambda h, j: (h, 0, 0)),
-            pl.BlockSpec((1, CLIPS, OWN, CHUNK), lambda h, j: (h, 0, 0, 0)),
+            pl.BlockSpec((1, OWN, CLIPS * HEAD), lambda j: (0, 0, 0)),
+            pl.BlockSpec((1, OWN, CHUNK), lambda j: (0, 0, 0)),
+            pl.BlockSpec((1, CLIPS, OWN, CHUNK), lambda j: (0, 0, 0, 0)),
         ],
         out_shape=[
-            jax.ShapeDtypeStruct((2, OWN, CLIPS * HEAD), jnp.float32),
-            jax.ShapeDtypeStruct((2, OWN, CHUNK), jnp.float32),
-            jax.ShapeDtypeStruct((2, CLIPS, OWN, CHUNK), jnp.float32),
-        ],
-        cost_estimate=pl.CostEstimate(flops=25 * 10**9, bytes_accessed=25 * 10**6, transcendentals=17 * 10**6),
+            jax.ShapeDtypeStruct((1, OWN, CLIPS * HEAD), jnp.float32),
+            jax.ShapeDtypeStruct((1, OWN, CHUNK), jnp.float32),
+            jax.ShapeDtypeStruct((1, CLIPS, OWN, CHUNK), jnp.float32),
+        ],
+        cost_estimate=pl.CostEstimate(flops=20 * 10**9, bytes_accessed=15 * 10**6, transcendentals=9 * 10**6),
         name="masked_queries",
     )(q, k, v4, keep_rows)
 
@@ -237,58 +299,47 @@
 
 
 def join_kernel(qb_ref, qv_ref, kv_ref, accb_ref, mb_ref, lb_ref, accv_ref, mv_ref, lv_ref, place_ref, out_ref):
-    clip = pl.program_id(0)
+    clip, head = pl.program_id(0), pl.program_id(1)
     lanes = lax.broadcasted_iota(jnp.int32, (1, 2 * HEAD), 1)
     k = kv_ref[:, 0, :, : 2 * HEAD].reshape(VIS, 2 * HEAD)
     v = kv_ref[:, 0, :, 2 * HEAD :].reshape(VIS, 2 * HEAD)
     place = place_ref[0]
     seen = jnp.sum(place, axis=1, keepdims=True) > 0.5
-    for head in range(2):
-        mine = (lanes // HEAD) == head
-        vis = join(
-            qv_ref[head, 0], k, v, own_columns(accv_ref[head, 0], clip, head), mv_ref[head, 0], lv_ref[head, 0]
-        ).astype(jnp.bfloat16)
-        for start in range(0, OWN, JOIN_ROWS):
-            rows = pl.ds(start, JOIN_ROWS)
-            base = join(
-                qb_ref[head, rows, :],
-                k,
-                v,
-                own_columns(accb_ref[head, rows, :], clip, head),
-                mb_ref[head, 0, rows, :],
-                lb_ref[head, 0, rows, :],
-            )
-            spread = jnp.dot(
-                place[start : start + JOIN_ROWS].astype(jnp.bfloat16), vis, preferred_element_type=jnp.float32
-            )
-            value = jnp.where(seen[start : start + JOIN_ROWS], spread, base).astype(jnp.bfloat16)
-            if head == 0:
-                out_ref[0, rows, :] = value
-            else:
-                out_ref[0, rows, :] = jnp.where(mine, value, out_ref[0, rows, :])
+    vis = join(qv_ref[0, 0], k, v, own_columns(accv_ref[0, 0], clip, head), mv_ref[0, 0], lv_ref[0, 0])
+    base = join(qb_ref[0], k, v, own_columns(accb_ref[0], clip, head), mb_ref[0, 0], lb_ref[0, 0])
+    spread = jnp.dot(place.astype(jnp.bfloat16), vis.astype(jnp.bfloat16), preferred_element_type=jnp.float32)
+    value = jnp.where(seen, spread, base).astype(jnp.bfloat16)
+
+    @pl.when(head == 0)
+    def _():
+        out_ref[0] = value
+
+    @pl.when(head == 1)
+    def _():
+        out_ref[0] = jnp.where(lanes >= HEAD, value, out_ref[0])
 
 
 def join_attention(qb, qv, kv, base, single, place):
     seq_count = kv.shape[0]
     accb, mb, lb = base
     accv, mv, lv = [x.reshape(2, CLIPS, OWNVIS, -1) for x in single]
-    vis_spec = lambda width: pl.BlockSpec((2, 1, OWNVIS, width), lambda c: (0, c, 0, 0))
+    vis_spec = lambda width: pl.BlockSpec((1, 1, OWNVIS, width), lambda c, h: (h, c, 0, 0))
     return pl.pallas_call(
         join_kernel,
-        grid=(CLIPS,),
+        grid=(CLIPS, 2),
         in_specs=[
-            pl.BlockSpec((2, OWN, 2 * HEAD), lambda c: (0, 0, 0)),
+            pl.BlockSpec((1, OWN, 2 * HEAD), lambda c, h: (h, 0, 0)),
             vis_spec(2 * HEAD),
-            pl.BlockSpec((seq_count, 1, OWNVIS, 4 * HEAD), lambda c: (0, c, 0, 0)),
-            pl.BlockSpec((2, OWN, CLIPS * HEAD), lambda c: (0, 0, 0)),
-            pl.BlockSpec((2, 1, OWN, CHUNK), lambda c: (0, c, 0, 0)),
-            pl.BlockSpec((2, 1, OWN, CHUNK), lambda c: (0, c, 0, 0)),
+            pl.BlockSpec((seq_count, 1, OWNVIS, 4 * HEAD), lambda c, h: (0, c, 0, 0)),
+            pl.BlockSpec((1, OWN, CLIPS * HEAD), lambda c, h: (h, 0, 0)),
+            pl.BlockSpec((1, 1, OWN, CHUNK), lambda c, h: (h, c, 0, 0)),
+            pl.BlockSpec((1, 1, OWN, CHUNK), lambda c, h: (h, c, 0, 0)),
             vis_spec(CLIPS * HEAD),
             vis_spec(CHUNK),
             vis_spec(CHUNK),
-            pl.BlockSpec((1, OWN, OWNVIS), lambda c: (c, 0, 0)),
-        ],
-        out_specs=pl.BlockSpec((1, OWN, 2 * HEAD), lambda c: (c, 0, 0)),
+            pl.BlockSpec((1, OWN, OWNVIS), lambda c, h: (c, 0, 0)),
+        ],
+        out_specs=pl.BlockSpec((1, OWN, 2 * HEAD), lambda c, h: (c, 0, 0)),
         out_shape=jax.ShapeDtypeStruct((CLIPS, OWN, 2 * HEAD), jnp.bfloat16),
         cost_estimate=pl.CostEstimate(flops=8 * 10**9, bytes_accessed=10**7, transcendentals=7 * 10**6),
         name="join_visible_keys",
@@ -337,10 +388,11 @@
     )(x, gain, bias, w)
 
 
-def encoder_kernel(q_ref, kv_ref, offset_ref, turn_ref, proj_ref, out_ref, context_ref):
+def encoder_kernel(q_ref, own_ref, others_ref, offset_ref, turn_ref, proj_ref, out_ref, context_ref):
     width = q_ref.shape[1]
     head_size = D // HEADS
     scale = LOG2E / math.sqrt(head_size)
+    members = [own_ref] + [others_ref.at[g] for g in range(GROUP - 1)]
     sums = []
     for low, high, heads in ((0, 256, (0, 1)), (128, width, (2, 3))):
         lanes = lax.broadcasted_iota(jnp.int32, (1, high - low), 1) + low
@@ -349,7 +401,7 @@
         for head in heads:
             mine = (lanes >= head * head_size) & (lanes < (head + 1) * head_size)
             q = jnp.where(mine, window, jnp.zeros_like(window))
-            s = [jnp.dot(q, kv_ref[g, 0, low:high, :], preferred_element_type=jnp.float32) for g in range(GROUP)]
+            s = [jnp.dot(q, members[g][0, low:high, :], preferred_element_type=jnp.float32) for g in range(GROUP)]
             s = jnp.concatenate(s, axis=1) * scale + offset_ref[...]
             e = jnp.exp2(s - jnp.max(s, axis=1, keepdims=True))
             total = jnp.sum(lane_tiles(e), axis=1, keepdims=True)
@@ -358,7 +410,7 @@
             for g in range(GROUP):
                 piece = lax.dot_general(
                     e[:, g * SLOTS : (g + 1) * SLOTS],
-                    kv_ref[g, 1, low:high, :],
+                    members[g][1, low:high, :],
                     NT,
                     preferred_element_type=jnp.float32,
                 )
@@ -374,19 +426,16 @@
     out_ref[...] = jnp.dot(turned, proj_ref[...], preferred_element_type=jnp.float32).astype(jnp.bfloat16)
 
 
-def encoder_attention(q, kv, offset, turn, proj):
+def encoder_attention(q, own, others, offset, turn, proj):
     return pl.pallas_call(
         encoder_kernel,
-        in_specs=[pl.BlockSpec(memory_space=pltpu.VMEM)] * 5,
+        in_specs=[pl.BlockSpec(memory_space=pltpu.VMEM)] * 6,
         out_specs=pl.BlockSpec(memory_space=pltpu.VMEM),
         out_shape=jax.ShapeDtypeStruct((q.shape[0], D), jnp.bfloat16),
         scratch_shapes=[pltpu.VMEM(q.shape, jnp.bfloat16)],
         cost_estimate=pl.CostEstimate(flops=9 * 10**9, bytes_accessed=5 * 10**6, transcendentals=5 * 10**6),
         name="encoder_attention",
-    )(q, kv, offset, turn, proj)
-
-
-MESH = pl.DeviceIdType.MESH
+    )(q, own, others, offset, turn, proj)
 
 
 def finish_kernel(groups, parts_ref, tokens_ref, gain_ref, bias_ref, dec_ref, out_ref, got, send, recv):
@@ -540,9 +589,10 @@
     before = lax.dynamic_slice(starts, (clip_index, member), (1, 1))[0, 0]
 
     enc_q, enc_kv = encoder_projections(vis_tokens, enc_gain, enc_bias, jnp.swapaxes(enc_qkv, 1, 2))
-    groups = [[clip + CLIPS * g for g in range(GROUP)] for clip in range(CLIPS)]
-    group_kv = lax.all_gather(enc_kv, "seq", axis_index_groups=groups)
-    live = (slot_ids[None, :] < group_counts[:, None]).reshape(1, GROUP * SLOTS)
+    before_ids = (member - jnp.arange(GROUP, dtype=jnp.int32)) % GROUP
+    near = before_ids[:, None] == jnp.arange(GROUP, dtype=jnp.int32)[None, :]
+    near_counts = jnp.sum(jnp.where(near, group_counts[None, :], 0), axis=1)
+    live = (slot_ids[None, :] < near_counts[:, None]).reshape(1, GROUP * SLOTS)
 
     frame_ids = jnp.arange(S, dtype=jnp.int32)
     flags = jnp.any(vis_spatial[:, :, None] == frame_ids[None, None, :], axis=1)
@@ -554,7 +604,6 @@
     offset_rows = (1.0 - keep_rows) * floor_score
     offsets = jnp.repeat(offset_rows, OWNVIS, axis=1)
     wkv = jnp.concatenate([dec_qkv[1], dec_qkv[2]], axis=1)
-    k_masked, v_masked = make_tables(mask_token, dec_gain, dec_bias, wkv, keep)
 
     own_ids = jnp.arange(OWN, dtype=jnp.int32)
     own_frame, own_place = own_ids // BLOCK, own_ids % BLOCK
@@ -574,32 +623,16 @@
     q_masked = split_heads(jnp.dot(base_in, dec_qkv[0], preferred_element_type=jnp.float32))
     b1, b2 = b1[BLOCK:].reshape(CLIPS, 1, VB, DD), b2[BLOCK:].reshape(CLIPS, 1, VB, DD)
     vis_table = a1[None, :, None, :] * b1 + a2[None, :, None, :] * b2
-    base = base_attention(q_masked, k_masked, v_masked, keep_rows)
+    k_masked, v_masked, *base, others = masked_part(
+        mask_token, dec_gain, dec_bias, wkv, keep, q_masked[:1], keep_rows, enc_kv
+    )
     source = (slot_ids - before) % SLOTS
     turn = (source[:, None] == slot_ids[None, :]).astype(jnp.bfloat16)
     turn_part = lax.dynamic_slice_in_dim(turn, quarter * QUARTER, QUARTER, 0)
     tokens_part = jnp.dot(turn_part, vis_tokens, preferred_element_type=jnp.float32)
-    group_kv, base, tokens_part, vis_table, turn = lax.optimization_barrier(
-        (group_kv, base, tokens_part, vis_table, turn)
-    )
-
-    def by_clip(_):
-        offset = jnp.broadcast_to(
-            offset_rows.transpose(1, 0, 2)[:, :, None, :], (CLIPS, CHUNKS, SLOW_ROWS, CHUNK)
-        )
-        accs, ms, ls = lax.map(lambda x: single_attention(q_masked, k_masked, v_masked, x, SLOW_ROWS), offset)
-        acc = accs[0]
-        for clip in range(1, CLIPS):
-            acc = jnp.where(lane_clip[None, None, :] == clip, accs[clip], acc)
-        return acc, jnp.swapaxes(ms, 0, 1), jnp.swapaxes(ls, 0, 1)
-
-    def shared(_):
-        return base[0], jnp.broadcast_to(base[1][:, None], (2, CLIPS, OWN, CHUNK)), base[2]
-
-    vanishing = jnp.min(jnp.sum(base[2], axis=-1)) < 2.0**-60
-    base = lax.cond(vanishing, by_clip, shared, None)
-
-    parts = encoder_attention(enc_q, group_kv, jnp.where(live, 0.0, floor_score), turn, enc_proj)
+    tokens_part, vis_table, turn = lax.optimization_barrier((tokens_part, vis_table, turn))
+
+    parts = encoder_attention(enc_q, enc_kv, others, jnp.where(live, 0.0, floor_score), turn, enc_proj)
     encoded = finish_encoder(parts, tokens_part, final_gain, final_bias, to_decoder)
 
     groups = lax.axis_size("head")
@@ -625,6 +658,27 @@
     vis_kv = jnp.concatenate([vis_k, vis_v], axis=1).astype(jnp.bfloat16).reshape(CLIPS, OWNVIS, 4 * HEAD)
     all_kv = lax.all_gather(vis_kv, "seq")
     q_visible = split_heads(vis_q)
+
+    def by_clip(_):
+        offset = jnp.broadcast_to(
+            offset_rows.transpose(1, 0, 2)[:, :, None, :], (CLIPS, CHUNKS, SLOW_ROWS, CHUNK)
+        )
+        accs, ms, ls = lax.map(lambda x: single_attention(q_masked, k_masked, v_masked, x, SLOW_ROWS), offset)
+        acc = accs[0]
+        for clip in range(1, CLIPS):
+            acc = jnp.where(lane_clip[None, None, :] == clip, accs[clip], acc)
+        return acc, jnp.swapaxes(ms, 0, 1), jnp.swapaxes(ls, 0, 1)
+
+    later, _ = lax.optimization_barrier((q_masked[1:], vis_kv))
+    second = base_attention(1, later, k_masked, v_masked, keep_rows)
+    base = [jnp.concatenate([x, y]) for x, y in zip(base, second)]
+
+    def shared(_):
+        return base[0], jnp.broadcast_to(base[1][:, None], (2, CLIPS, OWN, CHUNK)), base[2]
+
+    vanishing = jnp.min(jnp.sum(base[2], axis=-1)) < 2.0**-60
+    base = lax.cond(vanishing, by_clip, shared, None)
+
     single = single_attention(q_visible, k_masked, v_masked, offsets, CLIPS * OWNVIS)
 
     token_ids = jnp.arange(OWNVIS, dtype=jnp.int32)

time: 217 us -> 251 us (1.16)
  Pallas kernels: 154 us -> 198 us
  waiting for transfers between devices: 21.5 us -> 0.02 us
  local copies, waits for them, and re-layouts: 7.8 us -> 13.6 us
  other arithmetic: 14.9 us -> 19.3 us
    pallas_call x3, Pallas kernels: 76.9 us -> 112 us  [the longest x1 72.6 us: masked_part(): pl.pallas_call(masked_kernel, grid=(CHUNKS,), in_specs=[pl.BlockSpec((1,...]
    all_gather x1, waiting for transfers between devices: 18.5 us -> 0.01 us  [body(): all_kv = lax.all_gather(vis_kv, 'seq')]
    pallas_call x1, Pallas kernels: 21.2 us -> 30 us  [hand_over(): pl.pallas_call(lambda *refs: hand_over_kernel(count, groups, *refs), in_s...]
    all_gather x1 -> x0, waiting for transfers between devices: 2.97 us -> none  [body(): group_kv = lax.all_gather(enc_kv, 'seq', axis_index_groups=groups)]
  transfers between devices with their start and end apart: 2 -> 1, of which waited for: 2 -> 0; matrix products, arithmetic and copies ran while one was open for 10% -> 5% of each run, Pallas kernels for 35% -> 14%
where the time goes in v4:
time: 251 us; the launch traced here: 250 us
  Pallas kernels  198 us (79%)
  other arithmetic  19.3 us (8%)
  between operations  14.5 us (6%)
  local copies, waits for them, and re-layouts  13.6 us (5%)
  matrix products  4.07 us (2%)
    pallas_call x1, Pallas kernels, masked_part(): pl.pallas_call(masked_kernel, grid=(CHUNKS,), in_specs=[pl.BlockSpec((1,...  72.6 us
    pallas_call x1, Pallas kernels, hand_over(): pl.pallas_call(lambda *refs: hand_over_kernel(count, groups, *refs), in_s...  30 us
    pallas_call x1, Pallas kernels, join_attention(): pl.pallas_call(join_kernel, grid=(CLIPS, 2), in_specs=[pl.BlockSpec((1, O...  20.4 us
    pallas_call x1, Pallas kernels, finish_encoder(): pl.pallas_call(lambda *refs: finish_kernel(groups, *refs), in_specs=[pl.B...  18.8 us
    pallas_call x1, Pallas kernels, base_attention(): pl.pallas_call(base_kernel, grid=(CHUNKS,), in_specs=[pl.BlockSpec((1, OW...  18.7 us
    pallas_call x1, Pallas kernels, single_attention(): pl.pallas_call(single_kernel, grid=(blocks, CHUNKS), in_specs=[pl.BlockSp...  17.4 us
    pallas_call x1, Pallas kernels, encoder_attention(): pl.pallas_call(encoder_kernel, in_specs=[pl.BlockSpec(memory_space=pltpu....  14.4 us
    pallas_call x1, Pallas kernels, encoder_projections(): pl.pallas_call(project_kernel, grid=(3,), in_specs=[pl.BlockSpec((slots,...  5.94 us
  transfers between devices with their start and end apart: 1, of which 0 were waited for; matrix products, arithmetic and copies ran while one was open for 5% of the time, Pallas kernels for 14%

profile of v4, /device:TPU:1, one launch (start us, length us, event | category | flops | bytes accessed | tf_op | source)
XLA Modules:
  0.0 249.8 jit_solution(10697419721542267221)
XLA Ops:
  6.6 1.1 fusion.5
  7.7 0.8 broadcast_subtract_fusion
  9.4 0.9 fusion.11
  10.3 1.0 multiply_reduce_fusion
  11.4 1.0 slice_bitcast_fusion.1
  12.4 1.1 add_convert_fusion
  14.3 0.7 fusion.58
  15.1 2.8 %multiply_sine_fusion = (f32[128,512]{1,0:T(8,128)}, f32[128,512]{1,0:T(8,128)}, f32[128,512]{1,0:T(8,128)}, f32[128,512]{1,0:T(8,128)}) fusion(f32[128]{0:T(128)S(1)} %iota_convert_fusion, f32[512]{0:T(512)S(1)} %fusion.41, f32[128]{0:T(128)S(1)} %convert_element_type.109, pred[512]{0:T(512)(128)(4,1)S(1)} %fusion.36), kind=kLoop, calls=%fused_computation.37 | loop fusion | flops 327680 | bytes 1052160 | tf_op jit(solution)/shard_map/sin | solution.py:131
  18.5 1.7 fusion.29
  21.7 0.9 fusion.31
  22.7 1.1 fusion.16.refs_1_
  24.8 0.7 pad_maximum_fusion.2.wkv
  25.5 5.9 %encoder_projections.1 = (bf16[384,352]{1,0:T(8,128)(2,1)}, bf16[2,352,384]{2,1,0:T(8,128)(2,1)}) custom-call(bf16[384,1408]{1,0:T(8,128)(2,1)} %x_ref.1, f32[1408]{0:T(1024)} %gain_ref.1, f32[1408]{0:T(1024)} %bias_ref.1, bf16[3,352,1408]{2,1,0:T(8,128)(2,1)} %bitcast.107), custom_call_target="tpu_custom_call" | custom-call | flops 1200000000 | bytes 5000000 | tf_op jit(solution)/shard_map/encoder_projections/pallas_call | solution.py:368
  31.4 72.6 %masked_part.1 = (bf16[16384,128]{1,0:T(8,128)(2,1)}, bf16[2,16384,256]{2,1,0:T(8,128)(2,1)}, f32[1,512,256]{2,1,0:T(8,128)}, f32[1,512,128]{2,1,0:T(8,128)}, f3...) custom-call(f32[8,16,512]{2,1,0:T(8,128)} %bitcast.98, f32[8,16,512]{2,1,0:T(8,128)} %bitcast.99, ...), custom_call_target="tpu_custom_call" | custom-call | flops 40000000000 | bytes 35000000 | tf_op jit(solution)/shard_map/masked_part/pallas_call | solution.py:139
  104.1 14.4 %encoder_attention.1 = bf16[384,1408]{1,0:T(8,128)(2,1)} custom-call(bf16[384,352]{1,0:T(8,128)(2,1)} %get-tuple-element.137.q_ref, bf16[2,352,384]{2,1,0:T(8,128)(2,1)} %get-tuple-element.138.kv_ref.own_ref, bf16[7,2,352,384]{3,2,1,0:T(8,128)(2,1)} %get-tuple-element.143.others_ref, f32[1,3072]{1,0:T(1,128)} %bitcast.103, ...), custom_call_target="tpu_custom_call" | custom-call | flops 8999999488 | bytes 5000000 | tf_op jit(solution)/shard_map/encoder_attention/pallas_call | solution.py:430
  118.5 18.8 %finish_encoder.1 = bf16[96,512]{1,0:T(8,128)(2,1)} custom-call(bf16[4,96,1408]{2,1,0:T(8,128)(2,1)} %bitcast.94, f32[96,1408]{1,0:T(8,128)} %fusion.16.refs_1_, f32[1408]{0:T(1024)} %refs_2_.1, f32[1408]{0:T(1024)} %refs_3_.1, bf16[1408,512]{1,0:T(8,128)(2,1)} %refs_4_.1), custom_call_target="tpu_custom_call" | custom-call | flops 200000000 | bytes 3000000 | tf_op jit(solution)/shard_map/finish_encoder/pallas_call | solution.py:472
  137.3 1.0 reshape.628
  138.3 0.7 pad.4.refs_0_
  139.0 30.0 %hand_over.1 = bf16[4,32,16,128]{3,2,1,0:T(8,128)(2,1)} custom-call(bf16[32,16,128]{2,1,0:T(8,128)(2,1)} %pad.4.refs_0_), custom_call_target="tpu_custom_call" | custom-call | tf_op jit(solution)/shard_map/hand_over/pallas_call | solution.py:548
  169.0 1.4 reshape.629
  173.5 0.7 pad_maximum_fusion.3
  174.2 1.3 constant_dynamic-update-slice_fusion.1
  175.5 18.7 %masked_queries.1 = (f32[1,512,256]{2,1,0:T(8,128)}, f32[1,512,128]{2,1,0:T(8,128)}, f32[1,4,512,128]{3,2,1,0:T(8,128)}) custom-call(bf16[1,512,128]{2,1,0:T(8,128)(2,1)} %get-tuple-element.238.q_ref, bf16[16384,128]{1,0:T(8,128)(2,1)} %get-tuple-element.147.k_ref, bf16[2,16384,256]{2,1,0:T(8,128)(2,1)} %get-tuple-element.148.v_ref, ...), custom_call_target="tpu_custom_call" | custom-call | flops 20000000000 | bytes 15000000 | tf_op jit(solution)/shard_map/masked_queries/pallas_call | solution.py:217
  194.2 1.4 constant_dynamic-update-slice_fusion
  197.6 2.2 pad_maximum_fusion
  199.9 1.5 conditional.1
  199.9 1.4 broadcast_in_dim.104.clone
  202.4 0.7 broadcast_select_fusion.2.qv_ref
  203.0 1.2 and_convert_fusion.place_ref
  204.2 0.9 broadcast_in_dim.243
  205.2 17.4 %visible_queries.1 = (f32[2,192,256]{2,1,0:T(8,128)}, f32[2,192,128]{2,1,0:T(8,128)}, f32[2,192,128]{2,1,0:T(8,128)}) custom-call(bf16[2,192,128]{2,1,0:T(8,128)(2,1)} %broadcast_select_fusion.1.q_ref, bf16[16384,128]{1,0:T(8,128)(2,1)} %get-tuple-element.147.k_ref, bf16[2,16384,256]{2,1,0:T(8,128)(2,1)} %get-tuple-element.148.v_ref, f32[8,192,128]{2,1,0:T(8,128)} %bitcast.96), custom_call_target="tpu_custom_call" | custom-call | flops 20000000000 | bytes 25000000 | tf_op jit(solution)/shard_map/visible_queries/pallas_call | solution.py:266
  222.5 20.4 %join_visible_keys.1 = bf16[4,512,128]{2,1,0:T(8,128)(2,1)} custom-call(bf16[2,512,128]{2,1,0:T(8,128)(2,1)S(1)} %broadcast_select_fusion.qb_ref, bf16[2,4,48,128]{3,2,1,0:T(8,128)(2,1)} %broadcast_select_fusion.2.qv_ref, bf16[32,4,48,256]{3,2,1,0:T(8,128)(2,1)} %all-gather.2.cloned.1.call-done.kv_ref, f32[2,512,256]{2,1,0:T(8,128)} %get-tuple-element.154.accb_ref, ...), custom_call_target="tpu_custom_call" | custom-call | flops 8000000000 | bytes 10000000 | tf_op jit(solution)/shard_map/join_visible_keys/pallas_call | solution.py:327
  (98 shorter events, 10.3 us)
Async XLA Ops:
  6.5 6.9 %copy-start.2 = (bf16[3,512,128]{2,1,0:T(8,128)(2,1)S(1)}, bf16[3,512,128]{2,1,0:T(8,128)(2,1)}, u32[]{:S(2)}) copy-start(bf16[3,512,128]{2,1,0:T(8,128)(2,1)} %param.31) | copy-start | bytes 1179652
  6.5 216.0 %all-gather.2.cloned.1.call-start = ((), (), s32[]{:S(2)}) async-start(), calls=%async_computation | async-start | bytes 3244032 | tf_op jit(solution)/shard_map/all_gather | solution.py:659
  13.4 6.8 %copy-start.6 = (s32[4,8]{1,0:T(4,128)S(1)}, s32[4,8]{1,0:T(4,128)}, u32[]{:S(2)}) copy-start(s32[4,8]{1,0:T(4,128)} %param.19) | copy-start | bytes 388
  13.8 0.5 copy-start.9
  13.8 8.9 %copy-start.3 = (bf16[384,1408]{1,0:T(8,128)(2,1)S(1)}, bf16[384,1408]{1,0:T(8,128)(2,1)}, u32[]{:S(2)}) copy-start(bf16[384,1408]{1,0:T(8,128)(2,1)} %x_ref.1) | copy-start | bytes 3244036
  169.0 4.0 %copy-start.7 = (f32[512]{0:T(512)S(1)}, f32[512]{0:T(512)}, u32[]{:S(2)}) copy-start(f32[512]{0:T(512)} %param.30) | copy-start | bytes 6148
  169.0 4.0 %copy-start.8 = (f32[512]{0:T(512)S(1)}, f32[512]{0:T(512)}, u32[]{:S(2)}) copy-start(f32[512]{0:T(512)} %param.29) | copy-start | bytes 6148
  194.2 3.3 %copy-start.4 = (f32[1,512,128]{2,1,0:T(8,128)S(1)}, f32[1,512,128]{2,1,0:T(8,128)}, u32[]{:S(2)}) copy-start(f32[1,512,128]{2,1,0:T(8,128)} %get-tuple-element.150) | copy-start | bytes 786436
  194.2 3.3 %copy-start.5 = (f32[1,512,128]{2,1,0:T(8,128)S(1)}, f32[1,512,128]{2,1,0:T(8,128)}, u32[]{:S(2)}) copy-start(f32[1,512,128]{2,1,0:T(8,128)} %get-tuple-element.151) | copy-start | bytes 786436
  199.9 1.8 copy-start.10
Sparse Core Ops, SparseCore 0:
  174.3 44.0 all-gather.1

commit v5 on v3

--- a/solution.py
+++ b/solution.py
@@ -58,17 +58,23 @@
 
 def table_kernel(a1, a2, b1, b2, token, gain, bias, wkv, keep, k_ref, v_ref):
     lanes = lax.broadcasted_iota(jnp.int32, (1, 2 * HEAD), 1)
-    for tile in range(TILES):
-        rows = pl.ds(tile * CHUNK, CHUNK)
-        x = a1[0, tile : tile + 1, :] * b1[...] + a2[0, tile : tile + 1, :] * b2[...] + token[...]
-        h = layer_norm(x, gain[...], bias[...]).astype(jnp.bfloat16)
-        kv = jnp.dot(h, wkv[...], preferred_element_type=jnp.float32)
-        k_ref[rows, :] = kv[:, : 2 * HEAD].astype(jnp.bfloat16)
-        v = kv[:, 2 * HEAD :]
-        turned = pltpu.roll(v, HEAD, 1)
-        for head in range(2):
-            twice = jnp.where((lanes < HEAD) == (head == 0), v, turned)
-            v_ref[head, rows, :] = (jnp.concatenate([twice, twice], axis=1) * keep[0]).astype(jnp.bfloat16)
+
+    def some(part, carry):
+        for unrolled in range(TILES // 2):
+            tile = part * (TILES // 2) + unrolled
+            rows, one = pl.ds(pl.multiple_of(tile * CHUNK, CHUNK), CHUNK), pl.ds(tile, 1)
+            x = a1[0, one, :] * b1[...] + a2[0, one, :] * b2[...] + token[...]
+            h = layer_norm(x, gain[...], bias[...]).astype(jnp.bfloat16)
+            kv = jnp.dot(h, wkv[...], preferred_element_type=jnp.float32)
+            k_ref[rows, :] = kv[:, : 2 * HEAD].astype(jnp.bfloat16)
+            v = kv[:, 2 * HEAD :]
+            turned = pltpu.roll(v, HEAD, 1)
+            for head in range(2):
+                twice = jnp.where((lanes < HEAD) == (head == 0), v, turned)
+                v_ref[head, rows, :] = (jnp.concatenate([twice, twice], axis=1) * keep[0]).astype(jnp.bfloat16)
+        return carry
+
+    lax.fori_loop(0, 2, some, 0)
 
 
 def angle_tables(coarse, fine):
@@ -124,7 +130,7 @@
 
 BASE_ROWS = 128
 JOIN_ROWS = 512
-SLOW_ROWS = 32
+SLOW_ROWS = 16
 
 
 def base_kernel(q_ref, k_ref, v_ref, keep_ref, acc_ref, m_ref, l_ref):
@@ -183,6 +189,10 @@
         l_ref[...] = jnp.zeros_like(l_ref)
         m_ref[...] = jnp.full_like(m_ref, floor_score)
 
+    single_chunk(q_ref, k_ref, v_ref, offset_ref, acc_ref, m_ref, l_ref)
+
+
+def single_chunk(q_ref, k_ref, v_ref, offset_ref, acc_ref, m_ref, l_ref):
     offset = jnp.concatenate([offset_ref[0]] * FRAMES, axis=1)
     for head in range(2):
         s = lax.dot_general(q_ref[head], k_ref[...], NT, preferred_element_type=jnp.float32) + offset
@@ -217,8 +227,139 @@
             jax.ShapeDtypeStruct((2, rows, CHUNK), jnp.float32),
         ],
         cost_estimate=pl.CostEstimate(flops=20 * 10**9, bytes_accessed=25 * 10**6, transcendentals=6 * 10**6),
-        name="visible_queries" if blocks == 1 else "masked_queries_by_clip",
+        name="masked_queries_by_clip",
     )(q, k, v4, offsets)
+
+
+SIDE = 4
+MESH = pl.DeviceIdType.MESH
+
+
+def spread_kernel(
+    q_ref, k_ref, v_ref, offset_ref, own_k, own_v, acc_ref, m_ref, l_ref, all_k, all_v, local, send_1, recv_1, send_2,
+    recv_2, send_3, recv_3,
+):
+    step = pl.program_id(1)
+    seq, head = lax.axis_index("seq"), lax.axis_index("head")
+    core = lax.rem(seq, 2)
+    x, y = seq // (2 * SIDE), lax.rem(seq // 2, SIDE)
+    arrays = ((0, own_k, all_k), (1, own_v, all_v))
+
+    def chip(kind, along, across):
+        a, b = (along, across) if kind == 0 else (across, along)
+        return lax.rem(x + a + SIDE, SIDE) * SIDE + lax.rem(y + b + SIDE, SIDE)
+
+    def remote(source, target, place, sends, recvs, index, peer_chip, peer_core):
+        return pltpu.make_async_remote_copy(
+            src_ref=source,
+            dst_ref=target.at[place, core],
+            send_sem=sends.at[index],
+            recv_sem=recvs.at[index],
+            device_id=(peer_chip * 2 + peer_core, head),
+            device_id_type=MESH,
+        )
+
+    def first(kind, own, whole, d):
+        return remote(own, whole, chip(kind, 0, 0), send_1, recv_1, kind * 3 + d - 1, chip(kind, d, 0), core)
+
+    def second(kind, own, whole, e, d):
+        place = chip(kind, -d, 0)
+        source = own if d == 0 else whole.at[place, core]
+        index = kind * 12 + (e - 1) * SIDE + d
+        return remote(source, whole, place, send_2, recv_2, index, chip(kind, 0, e), core)
+
+    def third(kind, own, whole, e, d):
+        place = chip(kind, -d, -e)
+        source = own if d == 0 and e == 0 else whole.at[place, core]
+        index = kind * 16 + e * SIDE + d
+        return remote(source, whole, place, send_3, recv_3, index, chip(kind, 0, 0), 1 - core)
+
+    def keep(kind, own, whole):
+        return pltpu.make_async_copy(own, whole.at[chip(kind, 0, 0), core], local.at[kind])
+
+    @pl.when(step == 0)
+    def _():
+        barrier = pltpu.get_barrier_semaphore()
+        for d in range(1, SIDE):
+            for kind in range(2):
+                peer = (chip(kind, d, 0) * 2 + core, head)
+                pl.semaphore_signal(barrier, inc=1, device_id=peer, device_id_type=MESH)
+        peer = (chip(0, 0, 0) * 2 + 1 - core, head)
+        pl.semaphore_signal(barrier, inc=1, device_id=peer, device_id_type=MESH)
+        pl.semaphore_wait(barrier, 7)
+        for kind, own, whole in arrays:
+            for d in range(1, SIDE):
+                first(kind, own, whole, d).start()
+            third(kind, own, whole, 0, 0).start()
+            keep(kind, own, whole).start()
+        acc_ref[...] = jnp.zeros_like(acc_ref)
+        l_ref[...] = jnp.zeros_like(l_ref)
+        m_ref[...] = jnp.full_like(m_ref, floor_score)
+
+    @pl.when(step == 3)
+    def _():
+        for kind, own, whole in arrays:
+            for d in range(1, SIDE):
+                first(kind, own, whole, d).wait()
+            for d in range(SIDE):
+                for e in range(1, SIDE):
+                    second(kind, own, whole, e, d).start()
+            for d in range(1, SIDE):
+                third(kind, own, whole, 0, d).start()
+
+    single_chunk(q_ref, k_ref, v_ref, offset_ref, acc_ref, m_ref, l_ref)
+
+    @pl.when(step == CHUNKS - 1)
+    def _():
+        for e in range(1, SIDE):
+            for d in range(SIDE):
+                for kind, own, whole in arrays:
+                    second(kind, own, whole, e, d).wait()
+                    third(kind, own, whole, e, d).start()
+        for kind, own, whole in arrays:
+            keep(kind, own, whole).wait()
+            for e in range(SIDE):
+                for d in range(SIDE):
+                    third(kind, own, whole, e, d).wait()
+
+
+def spread_attention(q, k, v4, offsets, own_k, own_v):
+    rows = q.shape[1]
+    out_spec = lambda width: pl.BlockSpec((2, rows, width), lambda r, j: (0, 0, 0))
+    everyone = jax.ShapeDtypeStruct((SIDE * SIDE, 2, *own_k.shape), jnp.bfloat16)
+    sems = lambda n: pltpu.SemaphoreType.DMA((n,))
+    *sums, all_k, all_v = pl.pallas_call(
+        spread_kernel,
+        grid=(1, CHUNKS),
+        in_specs=[
+            pl.BlockSpec((2, rows, 2 * HEAD), lambda r, j: (0, 0, 0)),
+            pl.BlockSpec((KEYS, 2 * HEAD), lambda r, j: (j, 0)),
+            pl.BlockSpec((2, KEYS, CLIPS * HEAD), lambda r, j: (0, j, 0)),
+            pl.BlockSpec((1, rows, CHUNK), lambda r, j: (j, 0, 0)),
+            pl.BlockSpec(memory_space=pltpu.VMEM),
+            pl.BlockSpec(memory_space=pltpu.VMEM),
+        ],
+        out_specs=[
+            out_spec(CLIPS * HEAD),
+            out_spec(CHUNK),
+            out_spec(CHUNK),
+            pl.BlockSpec(memory_space=pl.ANY),
+            pl.BlockSpec(memory_space=pl.ANY),
+        ],
+        out_shape=[
+            jax.ShapeDtypeStruct((2, rows, CLIPS * HEAD), jnp.float32),
+            jax.ShapeDtypeStruct((2, rows, CHUNK), jnp.float32),
+            jax.ShapeDtypeStruct((2, rows, CHUNK), jnp.float32),
+            everyone,
+            everyone,
+        ],
+        scratch_shapes=[sems(2), sems(6), sems(6), sems(24), sems(24), sems(32), sems(32)],
+        compiler_params=pltpu.CompilerParams(collective_id=2, has_side_effects=True),
+        cost_estimate=pl.CostEstimate(flops=20 * 10**9, bytes_accessed=25 * 10**6, transcendentals=6 * 10**6),
+        name="visible_queries",
+    )(q, k, v4, offsets, own_k, own_v)
+    shape = (2 * SIDE * SIDE, CLIPS, OWNVIS, 2 * HEAD)
+    return sums, all_k.reshape(shape), all_v.reshape(shape)
 
 
 def own_columns(acc, clip, head):
@@ -236,11 +377,11 @@
     return (acc * factor + update) / total
 
 
-def join_kernel(qb_ref, qv_ref, kv_ref, accb_ref, mb_ref, lb_ref, accv_ref, mv_ref, lv_ref, place_ref, out_ref):
+def join_kernel(qb_ref, qv_ref, k_ref, v_ref, accb_ref, mb_ref, lb_ref, accv_ref, mv_ref, lv_ref, place_ref, out_ref):
     clip = pl.program_id(0)
     lanes = lax.broadcasted_iota(jnp.int32, (1, 2 * HEAD), 1)
-    k = kv_ref[:, 0, :, : 2 * HEAD].reshape(VIS, 2 * HEAD)
-    v = kv_ref[:, 0, :, 2 * HEAD :].reshape(VIS, 2 * HEAD)
+    k = k_ref[:, 0].reshape(VIS, 2 * HEAD)
+    v = v_ref[:, 0].reshape(VIS, 2 * HEAD)
     place = place_ref[0]
     seen = jnp.sum(place, axis=1, keepdims=True) > 0.5
     for head in range(2):
@@ -268,8 +409,8 @@
                 out_ref[0, rows, :] = jnp.where(mine, value, out_ref[0, rows, :])
 
 
-def join_attention(qb, qv, kv, base, single, place):
-    seq_count = kv.shape[0]
+def join_attention(qb, qv, k, v, base, single, place):
+    seq_count = k.shape[0]
     accb, mb, lb = base
     accv, mv, lv = [x.reshape(2, CLIPS, OWNVIS, -1) for x in single]
     vis_spec = lambda width: pl.BlockSpec((2, 1, OWNVIS, width), lambda c: (0, c, 0, 0))
@@ -279,7 +420,8 @@
         in_specs=[
             pl.BlockSpec((2, OWN, 2 * HEAD), lambda c: (0, 0, 0)),
             vis_spec(2 * HEAD),
-            pl.BlockSpec((seq_count, 1, OWNVIS, 4 * HEAD), lambda c: (0, c, 0, 0)),
+            pl.BlockSpec((seq_count, 1, OWNVIS, 2 * HEAD), lambda c: (0, c, 0, 0)),
+            pl.BlockSpec((seq_count, 1, OWNVIS, 2 * HEAD), lambda c: (0, c, 0, 0)),
             pl.BlockSpec((2, OWN, CLIPS * HEAD), lambda c: (0, 0, 0)),
             pl.BlockSpec((2, 1, OWN, CHUNK), lambda c: (0, c, 0, 0)),
             pl.BlockSpec((2, 1, OWN, CHUNK), lambda c: (0, c, 0, 0)),
@@ -292,7 +434,7 @@
         out_shape=jax.ShapeDtypeStruct((CLIPS, OWN, 2 * HEAD), jnp.bfloat16),
         cost_estimate=pl.CostEstimate(flops=8 * 10**9, bytes_accessed=10**7, transcendentals=7 * 10**6),
         name="join_visible_keys",
-    )(qb, qv.reshape(2, CLIPS, OWNVIS, -1), kv, accb, mb, lb, accv, mv, lv, place)
+    )(qb, qv.reshape(2, CLIPS, OWNVIS, -1), k, v, accb, mb, lb, accv, mv, lv, place)
 
 
 def project_kernel(x_ref, gain_ref, bias_ref, w_ref, q_ref, kv_ref, h_ref):
@@ -622,17 +764,17 @@
     vis_in = vis_table.reshape(CLIPS * OWNVIS, DD) + own_encoded
     vis_in = layer_norm(vis_in, dec_gain, dec_bias).astype(jnp.bfloat16)
     vis_q, vis_k, vis_v = [jnp.dot(vis_in, dec_qkv[i], preferred_element_type=jnp.float32) for i in range(3)]
-    vis_kv = jnp.concatenate([vis_k, vis_v], axis=1).astype(jnp.bfloat16).reshape(CLIPS, OWNVIS, 4 * HEAD)
-    all_kv = lax.all_gather(vis_kv, "seq")
     q_visible = split_heads(vis_q)
-    single = single_attention(q_visible, k_masked, v_masked, offsets, CLIPS * OWNVIS)
+    single, all_k, all_v = spread_attention(
+        q_visible, k_masked, v_masked, offsets, vis_k.astype(jnp.bfloat16), vis_v.astype(jnp.bfloat16)
+    )
 
     token_ids = jnp.arange(OWNVIS, dtype=jnp.int32)
     token_place = jnp.repeat(own_spatial[:, None, :] - seq_index * BLOCK, FRAMES, axis=1).reshape(CLIPS, 1, OWNVIS)
     place = (own_frame[None, :, None] == (token_ids // VB)[None, None, :]) & (own_place[None, :, None] == token_place)
     place = place.astype(jnp.float32)
 
-    out = join_attention(q_masked, q_visible, all_kv, base, single, place)
+    out = join_attention(q_masked, q_visible, all_k, all_v, base, single, place)
     return out.reshape(CLIPS, FRAMES, BLOCK, 2 * HEAD)
 
 

time: 217 us -> 211 us (0.972)
  waiting for transfers between devices: 21.5 us -> 0.02 us
  Pallas kernels: 154 us -> 169 us
    all_gather x1 -> x0, waiting for transfers between devices: 18.5 us -> none  [body(): all_kv = lax.all_gather(vis_kv, 'seq')]
    pallas_call x1, Pallas kernels: 17.5 us -> 26 us  [spread_attention(): pl.pallas_call(spread_kernel, grid=(1, CHUNKS), in_specs=[pl.BlockSpec((2...]
    pallas_call x1, Pallas kernels: 22.4 us -> 25.8 us  [make_tables(): pl.pallas_call(table_kernel, grid=(steps,), in_specs=[pl.BlockSpec((1, TI...]
    all_gather x1, waiting for transfers between devices: 2.97 us -> 0.01 us  [body(): group_kv = lax.all_gather(enc_kv, 'seq', axis_index_groups=groups)]
    pallas_call x1, Pallas kernels: 18 us -> 20.8 us  [finish_encoder(): pl.pallas_call(lambda *refs: finish_kernel(groups, *refs), in_specs=[pl.B...]
  transfers between devices with their start and end apart: 2 -> 1, of which waited for: 2 -> 0; matrix products, arithmetic and copies ran while one was open for 10% -> 8% of each run, Pallas kernels for 35% -> 29%
where the time goes in v5:
time: 211 us
  Pallas kernels  169 us (80%)
  between operations  14.5 us (7%)
  other arithmetic  14.3 us (7%)
  local copies, waits for them, and re-layouts  7.57 us (4%)
  matrix products  5.21 us (2%)
    pallas_call x1, Pallas kernels, base_attention(): pl.pallas_call(base_kernel, grid=(2, CHUNKS), in_specs=[pl.BlockSpec((1,...  35.3 us
    pallas_call x1, Pallas kernels, spread_attention(): pl.pallas_call(spread_kernel, grid=(1, CHUNKS), in_specs=[pl.BlockSpec((2...  26 us
    pallas_call x1, Pallas kernels, make_tables(): pl.pallas_call(table_kernel, grid=(steps,), in_specs=[pl.BlockSpec((1, TI...  25.8 us
    pallas_call x1, Pallas kernels, hand_over(): pl.pallas_call(lambda *refs: hand_over_kernel(count, groups, *refs), in_s...  21.5 us
    pallas_call x1, Pallas kernels, finish_encoder(): pl.pallas_call(lambda *refs: finish_kernel(groups, *refs), in_specs=[pl.B...  20.8 us
    pallas_call x1, Pallas kernels, join_attention(): pl.pallas_call(join_kernel, grid=(CLIPS,), in_specs=[pl.BlockSpec((2, OWN...  19.5 us
    pallas_call x1, Pallas kernels, encoder_attention(): pl.pallas_call(encoder_kernel, in_specs=[pl.BlockSpec(memory_space=pltpu....  14.3 us
    pallas_call x1, Pallas kernels, encoder_projections(): pl.pallas_call(project_kernel, grid=(3,), in_specs=[pl.BlockSpec((slots,...  6.07 us
  transfers between devices with their start and end apart: 1, of which 0 were waited for; matrix products, arithmetic and copies ran while one was open for 8% of the time, Pallas kernels for 29%

profile of v5, /device:TPU:1, one launch (start us, length us, event | category | flops | bytes accessed | tf_op | source)
XLA Modules:
  0.0 211.0 jit_solution(6314584626561254535)
XLA Ops:
  6.5 6.1 %encoder_projections.1 = (bf16[384,352]{1,0:T(8,128)(2,1)}, bf16[2,352,384]{2,1,0:T(8,128)(2,1)}) custom-call(bf16[384,1408]{1,0:T(8,128)(2,1)} %x_ref.1, f32[1408]{0:T(1024)} %gain_ref.1, f32[1408]{0:T(1024)} %bias_ref.1, bf16[3,352,1408]{2,1,0:T(8,128)(2,1)} %bitcast.100), custom_call_target="tpu_custom_call" | custom-call | flops 1200000000 | bytes 5000000 | tf_op jit(solution)/shard_map/encoder_projections/pallas_call | solution.py:459
  13.7 0.4 multiply_sine_fusion.2
  14.7 0.4 multiply_reduce_fusion
  15.1 0.7 pad_maximum_fusion.wkv
  15.8 2.8 %multiply_sine_fusion = (f32[128,512]{1,0:T(8,128)}, f32[128,512]{1,0:T(8,128)}, f32[128,512]{1,0:T(8,128)}, f32[128,512]{1,0:T(8,128)}) fusion(f32[128]{0:T(128)S(1)} %iota_convert_fusion, f32[512]{0:T(512)S(1)} %fusion.35, f32[128]{0:T(128)S(1)} %convert_element_type.106, pred[512]{0:T(512)(128)(4,1)S(1)} %fusion.30), kind=kLoop, calls=%fused_computation.33 | loop fusion | flops 327680 | bytes 1052160 | tf_op jit(solution)/shard_map/sin | solution.py:87
  18.8 0.6 dynamic_slice.18
  19.7 0.6 copy.44
  21.8 0.4 add_convert_fusion
  22.5 1.6 fusion.23
  24.1 25.8 %masked_tables.1 = (bf16[16384,128]{1,0:T(8,128)(2,1)}, bf16[2,16384,256]{2,1,0:T(8,128)(2,1)}) custom-call(f32[16,8,512]{2,1,0:T(8,128)} %bitcast.90, f32[16,8,512]{2,1,0:T(8,128)} %bitcast.91, f32[128,512]{1,0:T(8,128)} %get-tuple-element.141.b1, f32[128,512]{1,0:T(8,128)} %get-tuple-element.142.b2, f32[1,512]{1,0:T(1,128)} %bitcast.93, ...), custom_call_target="tpu_custom_call" | custom-call | flops 20000000000 | bytes 25000000 | tf_op jit(solution)/shard_map/masked_tables/pallas_call | solution.py:97
  49.9 0.7 add_select_fusion.4
  50.6 0.6 select_bitcast_fusion.keep_ref
  51.4 0.9 fusion.25
  52.4 1.2 and_convert_fusion.place_ref
  53.6 1.1 fusion.14.refs_1_
  54.7 35.3 %masked_queries.1 = (f32[2,512,256]{2,1,0:T(8,128)}, f32[2,512,128]{2,1,0:T(8,128)S(1)}, f32[2,4,512,128]{3,2,1,0:T(8,128)}) custom-call(bf16[2,512,128]{2,1,0:T(8,128)(2,1)S(1)} %broadcast_select_fusion.q_ref.qb_ref, bf16[16384,128]{1,0:T(8,128)(2,1)} %get-tuple-element.143.k_ref, bf16[2,16384,256]{2,1,0:T(8,128)(2,1)} %get-tuple-element.144.v_ref, ...), custom_call_target="tpu_custom_call" | custom-call | flops 24999999488 | bytes 25000000 | tf_op jit(solution)/shard_map/masked_queries/pallas_call | solution.py:161
  90.2 14.3 %encoder_attention.1 = bf16[384,1408]{1,0:T(8,128)(2,1)} custom-call(bf16[384,352]{1,0:T(8,128)(2,1)} %get-tuple-element.149.q_ref, bf16[8,2,352,384]{3,2,1,0:T(8,128)(2,1)} %bitcast.99, f32[1,3072]{1,0:T(1,128)} %bitcast.95, bf16[384,384]{1,0:T(8,128)(2,1)} %get-tuple-element.151.turn_ref, bf16[352,1408]{1,0:T(8,128)(2,1)} %proj_ref.1), custom_call_target="tpu_custom_call" | custom-call | flops 8999999488 | bytes 5000000 | tf_op jit(solution)/shard_map/encoder_attention/pallas_call | solution.py:520
  104.5 20.8 %finish_encoder.1 = bf16[96,512]{1,0:T(8,128)(2,1)} custom-call(bf16[4,96,1408]{2,1,0:T(8,128)(2,1)} %bitcast.86, f32[96,1408]{1,0:T(8,128)} %fusion.14.refs_1_, f32[1408]{0:T(1024)} %refs_2_.1, f32[1408]{0:T(1024)} %refs_3_.1, bf16[1408,512]{1,0:T(8,128)(2,1)} %refs_4_.1), custom_call_target="tpu_custom_call" | custom-call | flops 200000000 | bytes 3000000 | tf_op jit(solution)/shard_map/finish_encoder/pallas_call | solution.py:565
  125.4 1.0 reshape.578
  126.4 0.7 pad.4.refs_0_
  127.1 21.5 %hand_over.1 = bf16[4,32,16,128]{3,2,1,0:T(8,128)(2,1)} custom-call(bf16[32,16,128]{2,1,0:T(8,128)(2,1)} %pad.4.refs_0_), custom_call_target="tpu_custom_call" | custom-call | tf_op jit(solution)/shard_map/hand_over/pallas_call | solution.py:641
  148.6 1.4 reshape.579
  150.0 0.4 fusion.51
  151.0 0.8 convolution_convert_fusion.1.own_v
  151.8 0.8 convolution_convert_fusion.2.own_k
  152.6 2.2 %reduce_sum.49 = f32[2,4,512]{2,1,0:T(4,128)S(1)} reduce(f32[2,4,512,128]{3,2,1,0:T(8,128)} %get-tuple-element.155, f32[]{:T(128)} %constant.222.clone.1), dimensions={3}, to_apply=%region_6.7 | reduce | flops 520192 | bytes 2113540 | tf_op jit(solution)/shard_map/reduce_sum | solution.py:741
  154.8 0.6 reduce_min.9
  156.1 0.7 broadcast_select_fusion.1.q_ref
  156.7 0.7 broadcast_select_fusion.2.qv_ref
  157.5 1.0 broadcast_in_dim.223
  158.5 26.0 %visible_queries.1 = (f32[2,192,256]{2,1,0:T(8,128)}, f32[2,192,128]{2,1,0:T(8,128)}, f32[2,192,128]{2,1,0:T(8,128)}, bf16[16,2,192,128]{3,2,1,0:T(8,128)(2,1)}, bf16[16,2,192,128]{3,2,1,0:T(8,128)(2,1)}) custom-call(bf16[2,192,128]{2,1,0:T(8,128)(2,1)} %broadcast_select_fusion.1.q_ref, bf16[16384,128]{1,0:T(8,128)(2,1)} %get-tuple-element.143.k_ref, ...), custom_call_target="tpu_custom_call" | custom-call | flops 20000000000 | bytes 25000000 | tf_op jit(solution)/shard_map/visible_queries/pallas_call | solution.py:331
  184.6 19.5 %join_visible_keys.1 = bf16[4,512,128]{2,1,0:T(8,128)(2,1)} custom-call(bf16[2,512,128]{2,1,0:T(8,128)(2,1)S(1)} %broadcast_select_fusion.q_ref.qb_ref, bf16[2,4,48,128]{3,2,1,0:T(8,128)(2,1)} %broadcast_select_fusion.2.qv_ref, bf16[32,4,48,128]{3,2,1,0:T(8,128)(2,1)} %bitcast.101, bf16[32,4,48,128]{3,2,1,0:T(8,128)(2,1)} %bitcast.102, ...), custom_call_target="tpu_custom_call" | custom-call | flops 8000000000 | bytes 10000000 | tf_op jit(solution)/shard_map/join_visible_keys/pallas_call | solution.py:417
  (90 shorter events, 5.1 us)
Async XLA Ops:
  6.5 83.5 %all-gather.3.cloned.1.call-start = ((), (), s32[]{:S(2)}) async-start(), calls=%async_computation | async-start | bytes 4866048 | tf_op jit(solution)/shard_map/all_gather | solution.py:686
  6.5 6.5 %copy-start.12 = (s32[4,96]{1,0:T(4,128)S(1)}, s32[4,96]{1,0:T(4,128)}, u32[]{:S(2)}) copy-start(s32[4,96]{1,0:T(4,128)} %param.20) | copy-start | bytes 4612
  6.5 7.0 %copy-start.7 = (s32[4,8]{1,0:T(4,128)S(1)}, s32[4,8]{1,0:T(4,128)}, u32[]{:S(2)}) copy-start(s32[4,8]{1,0:T(4,128)} %param.19) | copy-start | bytes 388
  6.5 7.8 %copy-start.6 = (f32[512]{0:T(512)S(1)}, f32[512]{0:T(512)}, u32[]{:S(2)}) copy-start(f32[512]{0:T(512)} %param.28) | copy-start | bytes 6148
  6.5 8.5 %copy-start.4 = (bf16[3,512,128]{2,1,0:T(8,128)(2,1)S(1)}, bf16[3,512,128]{2,1,0:T(8,128)(2,1)}, u32[]{:S(2)}) copy-start(bf16[3,512,128]{2,1,0:T(8,128)(2,1)} %param.31) | copy-start | bytes 1179652
  13.7 8.1 %copy-start.8 = (f32[512]{0:T(512)S(1)}, f32[512]{0:T(512)}, u32[]{:S(2)}) copy-start(f32[512]{0:T(512)} %param.30) | copy-start | bytes 6148
  13.7 8.1 %copy-start.10 = (f32[512]{0:T(512)S(1)}, f32[512]{0:T(512)}, u32[]{:S(2)}) copy-start(f32[512]{0:T(512)} %param.29) | copy-start | bytes 6148
  49.9 3.7 %copy-start.5 = (bf16[384,1408]{1,0:T(8,128)(2,1)S(1)}, bf16[384,1408]{1,0:T(8,128)(2,1)}, u32[]{:S(2)}) copy-start(bf16[384,1408]{1,0:T(8,128)(2,1)} %x_ref.1) | copy-start | bytes 3244036
  125.3 25.3 %copy-start.9 = (f32[512]{0:T(512)S(1)}, f32[512]{0:T(512)}, u32[]{:S(2)}) copy-start(f32[512]{0:T(512)} %param.30) | copy-start | bytes 6148
  125.4 25.3 %copy-start.11 = (f32[512]{0:T(512)S(1)}, f32[512]{0:T(512)}, u32[]{:S(2)}) copy-start(f32[512]{0:T(512)} %param.29) | copy-start | bytes 6148
Sparse Core Ops, SparseCore 0:
  12.8 75.2 all-gather.2
